TPU v7x, 32 devices: a whole 2x2x4 slice. The times are simulated.
32 devices in a mesh: ctx: 8 (over y, x, core), fsdp: 4 (over z).
Axes of the slice: x: 2, y: 2, z: 4, core: 2. Of those that a mesh axis runs over, the one named last changes fastest.
Arguments:
- tokens: bfloat16 [4, 4096, 768], P('fsdp', 'ctx'), may hold values from -6 to 6
- cotangent: bfloat16 [4, 4096, 768], P('fsdp', 'ctx'), may hold values from -6 to 6
- lengths: int32 [4, 4], P('fsdp'), may hold values from 1 to 2048, 4096 in all within a row
- dealing: int32 [4, 16], P('fsdp'), may hold values from 0 to 15, each once within a row
- qkv_weight: bfloat16 [768, 2304], P('fsdp'), may hold values from -0.21875 to 0.21875
- out_weight: bfloat16 [768, 768], P('fsdp'), may hold values from -0.21875 to 0.21875
- in_weight: bfloat16 [768, 3072], P('fsdp'), may hold values from -0.21875 to 0.21875
- back_weight: bfloat16 [3072, 768], P('fsdp'), may hold values from -0.109375 to 0.109375
- norm_gains: bfloat16 [3, 768], P(None, 'fsdp'), may hold values from 0.25 to 1.75
- shifts: bfloat16 [7, 768], P(None, 'fsdp'), may hold values from -1.796875 to 1.796875
- ffn_gain: bfloat16 [3072], P('fsdp'), may hold values from 0.25 to 1.75
- ffn_shifts: bfloat16 [2, 3072], P(None, 'fsdp'), may hold values from -1.796875 to 1.796875
Outputs:
- mixed_out: bfloat16 [4, 4096, 768], P('fsdp', 'ctx')
- input_grad: float32 [4, 4096, 768], P('fsdp', 'ctx')
- qkv_grad: float32 [768, 2304], P(('ctx', 'fsdp'))
- out_grad: float32 [768, 768], P(('ctx', 'fsdp'))
- in_grad: float32 [768, 3072], P(('ctx', 'fsdp'))
- back_grad: float32 [3072, 768], P(('ctx', 'fsdp'))
- gains_grad: float32 [3, 768], P(None, ('ctx', 'fsdp'))
- shifts_grad: float32 [7, 768], P(None, ('ctx', 'fsdp'))
- ffn_gain_grad: float32 [3072], P(('ctx', 'fsdp'))
- ffn_shifts_grad: float32 [2, 3072], P(None, ('ctx', 'fsdp'))
Inputs may be any that keep to these rules, and one draw needn't show every extreme that they name: `lengths`: each row sums to 4096 and its largest entry is exactly 2048. `dealing`: each row is a permutation of the group numbers.
All inputs are finite; a program needn't handle non-finite values.
Results may differ from a plain program's by a relative error of at most 0.018.
Values may be sent and summed in bfloat16 or wider, within the bound.
No kernel may reach another device: no remote copies, remote signals or barrier semaphores. Data moves between devices by JAX's collectives and lax.ppermute only.
A program may use at most 256 MiB of HBM per device.

v0:
```python
import math

import jax
import jax.numpy as jnp
from jax import lax
from jax.sharding import PartitionSpec as P

D = 768
H = 12
DH = 64


def layer_norm(values, gain, shift):
    average = jnp.mean(values, axis=-1, keepdims=True)
    centred = values - average
    variance = jnp.mean(centred * centred, axis=-1, keepdims=True)
    return centred * lax.rsqrt(variance + 1e-05) * gain + shift


def gelu_exact(values):
    return jax.nn.gelu(values, approximate=False)


def row_places(first_row, row_count, deal_row, bounds, group_rows):
    row_ids = first_row + jnp.arange(row_count, dtype=jnp.int32)
    group_ids = row_ids // group_rows
    onehot = (group_ids[:, None] == jnp.arange(deal_row.shape[0], dtype=jnp.int32)[None, :]).astype(
        jnp.int32
    )
    picked = jnp.sum(onehot * deal_row[None, :], axis=1)
    places = picked * group_rows + row_ids % group_rows
    segment = jnp.sum((places[:, None] >= bounds[None, :]).astype(jnp.int32), axis=1)
    return (places, segment)


def outer_sum(left, right):
    return lax.dot_general(
        left, right, (((0,), (0,)), ((), ())), preferred_element_type=jnp.float32
    )


def times_transposed(left, matrix):
    return lax.dot_general(
        left, matrix, (((1,), (1,)), ((), ())), preferred_element_type=jnp.float32
    )


def unpack(loaded):
    qkv_w, out_w, in_w, back_w, gains, shift_rows, ffn_gain, ffn_shift_rows = loaded
    return (
        qkv_w,
        out_w,
        in_w,
        back_w,
        gains.astype(jnp.float32),
        shift_rows.astype(jnp.float32),
        ffn_gain.astype(jnp.float32),
        ffn_shift_rows.astype(jnp.float32),
    )


def local(
    tokens,
    cotangent,
    lengths,
    dealing,
    qkv_weight,
    out_weight,
    in_weight,
    back_weight,
    norm_gains,
    shifts,
    ffn_gain,
    ffn_shifts,
):
    position = lax.axis_index("ctx")
    tok_rows = tokens.shape[1]
    group_rows = tok_rows // 2
    deal_row = dealing[0]
    bounds = jnp.cumsum(lengths[0])
    scaling = DH ** (-0.5)
    loaded = (
        lax.all_gather(qkv_weight, "fsdp", axis=0, tiled=True),
        lax.all_gather(out_weight, "fsdp", axis=0, tiled=True),
        lax.all_gather(in_weight, "fsdp", axis=0, tiled=True),
        lax.all_gather(back_weight, "fsdp", axis=0, tiled=True),
        lax.all_gather(norm_gains, "fsdp", axis=1, tiled=True),
        lax.all_gather(shifts, "fsdp", axis=1, tiled=True),
        lax.all_gather(ffn_gain, "fsdp", axis=0, tiled=True),
        lax.all_gather(ffn_shifts, "fsdp", axis=1, tiled=True),
    )
    qkv_w, out_w, in_w, back_w, gains, shift_rows, ffn_scale, ffn_shift_rows = unpack(loaded)
    inputs = tokens[0].astype(jnp.float32)
    normed = layer_norm(inputs, gains[0], shift_rows[0])
    normed_low = normed.astype(jnp.bfloat16)
    projected = jnp.dot(normed_low, qkv_w, preferred_element_type=jnp.float32)
    query = (projected[:, :D] + shift_rows[1]).astype(jnp.bfloat16)
    keyed = projected[:, D : 2 * D].astype(jnp.bfloat16)
    valued = (projected[:, 2 * D :] + shift_rows[2]).astype(jnp.bfloat16)
    query3 = query.reshape(tok_rows, H, DH)
    q_places, q_segment = row_places(position * tok_rows, tok_rows, deal_row, bounds, group_rows)

    def allowed_pairs(qp, qs, k_places, k_segment):
        return ((k_segment[None, :] == qs[:, None]) & (k_places[None, :] <= qp[:, None]))[None]

    initial = (
        jnp.full((H, tok_rows), -1e30, jnp.float32),
        jnp.zeros((H, tok_rows), jnp.float32),
        jnp.zeros((H, tok_rows, DH), jnp.float32),
    )
    key_rows = lax.all_gather(keyed, "ctx", axis=0, tiled=True)
    value_rows = lax.all_gather(valued, "ctx", axis=0, tiled=True)
    key_count = key_rows.shape[0]
    block_rows = 512
    block_count = key_count // block_rows
    k_places, k_segment = row_places(jnp.int32(0), key_count, deal_row, bounds, group_rows)
    stacked = (
        key_rows.reshape(block_count, block_rows, H, DH),
        value_rows.reshape(block_count, block_rows, H, DH),
        k_places.reshape(block_count, block_rows),
        k_segment.reshape(block_count, block_rows),
    )

    def visit_block(inner_state, pieces):
        maxima, totals, weighted = inner_state
        key3, value3, block_places, block_segment = pieces
        scores = (
            jnp.einsum("qhd,khd->hqk", query3, key3, preferred_element_type=jnp.float32) * scaling
        )
        allowed = allowed_pairs(q_places, q_segment, block_places, block_segment)
        masked = jnp.where(allowed, scores, -1e30)
        raised = jnp.maximum(maxima, jnp.max(masked, axis=-1))
        rescale = jnp.exp(maxima - raised)
        expo = jnp.where(allowed, jnp.exp(masked - raised[..., None]), 0.0)
        totals = totals * rescale + jnp.sum(expo, axis=-1)
        weighted = weighted * rescale[..., None] + jnp.einsum(
            "hqk,khd->hqd", expo.astype(jnp.bfloat16), value3, preferred_element_type=jnp.float32
        )
        return ((raised, totals, weighted), None)

    maxima, totals, weighted = lax.scan(visit_block, initial, stacked)[0]
    context3 = weighted / totals[..., None]
    log_total = maxima + jnp.log(totals)
    context = context3.transpose(1, 0, 2).reshape(tok_rows, D)
    inner = layer_norm(context, gains[1], shift_rows[3])
    inner_low = inner.astype(jnp.bfloat16)
    branch = jnp.dot(inner_low, out_w, preferred_element_type=jnp.float32) + shift_rows[4]
    middle = inputs + branch
    normed_two = layer_norm(middle, gains[2], shift_rows[5])
    normed_two_low = normed_two.astype(jnp.bfloat16)
    hidden = jnp.dot(normed_two_low, in_w, preferred_element_type=jnp.float32) + ffn_shift_rows[0]
    activated = gelu_exact(hidden)
    inner_two = layer_norm(activated, ffn_scale, ffn_shift_rows[1])
    inner_two_low = inner_two.astype(jnp.bfloat16)
    result = jnp.dot(inner_two_low, back_w, preferred_element_type=jnp.float32) + shift_rows[6]
    mixed_out = (middle + result).astype(jnp.bfloat16)
    loaded_back = (
        lax.all_gather(qkv_weight, "fsdp", axis=0, tiled=True),
        lax.all_gather(out_weight, "fsdp", axis=0, tiled=True),
        lax.all_gather(in_weight, "fsdp", axis=0, tiled=True),
        lax.all_gather(back_weight, "fsdp", axis=0, tiled=True),
        lax.all_gather(norm_gains, "fsdp", axis=1, tiled=True),
        lax.all_gather(shifts, "fsdp", axis=1, tiled=True),
        lax.all_gather(ffn_gain, "fsdp", axis=0, tiled=True),
        lax.all_gather(ffn_shifts, "fsdp", axis=1, tiled=True),
    )
    qkv_w, out_w, in_w, back_w, gains, shift_rows, ffn_scale, ffn_shift_rows = unpack(loaded_back)
    upstream = cotangent[0].astype(jnp.float32)
    result_low = cotangent[0]
    grad_back_w = outer_sum(inner_two_low, result_low)
    grad_back_bias = jnp.sum(result_low.astype(jnp.float32), axis=0)
    grad_inner_two = times_transposed(result_low, back_w)
    norm_pull = jax.vjp(layer_norm, activated, ffn_scale, ffn_shift_rows[1])[1]
    grad_activated, grad_ffn_gain, grad_ffn_shift = norm_pull(grad_inner_two)
    gelu_pull = jax.vjp(gelu_exact, hidden)[1]
    grad_hidden = gelu_pull(grad_activated)[0]
    hidden_low = grad_hidden.astype(jnp.bfloat16)
    grad_in_w = outer_sum(normed_two_low, hidden_low)
    grad_in_bias = jnp.sum(hidden_low.astype(jnp.float32), axis=0)
    grad_normed_two = times_transposed(hidden_low, in_w)
    second_pull = jax.vjp(layer_norm, middle, gains[2], shift_rows[5])[1]
    grad_middle_part, grad_gain_two, grad_shift_five = second_pull(grad_normed_two)
    grad_middle = upstream + grad_middle_part
    branch_low = grad_middle.astype(jnp.bfloat16)
    grad_out_w = outer_sum(inner_low, branch_low)
    grad_out_bias = jnp.sum(branch_low.astype(jnp.float32), axis=0)
    grad_inner = times_transposed(branch_low, out_w)
    inner_pull = jax.vjp(layer_norm, context, gains[1], shift_rows[3])[1]
    grad_context, grad_gain_one, grad_shift_three = inner_pull(grad_inner)
    context_grad_low = grad_context.astype(jnp.bfloat16).reshape(tok_rows, H, DH)
    delta = jnp.einsum("qhd,hqd->hq", context_grad_low.astype(jnp.float32), context3)

    def grad_pair(
        q_rows, grad_rows, lse_rows, delta_rows, qp, qs, key3, value3, k_places, k_segment
    ):
        scores = (
            jnp.einsum("qhd,khd->hqk", q_rows, key3, preferred_element_type=jnp.float32) * scaling
        )
        allowed = allowed_pairs(qp, qs, k_places, k_segment)
        probabilities = jnp.where(allowed, jnp.exp(scores - lse_rows[..., None]), 0.0)
        upstream_probs = jnp.einsum(
            "qhd,khd->hqk", grad_rows, value3, preferred_element_type=jnp.float32
        )
        score_grad = (probabilities * (upstream_probs - delta_rows[..., None])).astype(jnp.bfloat16)
        query_add = (
            jnp.einsum("hqk,khd->qhd", score_grad, key3, preferred_element_type=jnp.float32)
            * scaling
        )
        key_add = (
            jnp.einsum("hqk,qhd->khd", score_grad, q_rows, preferred_element_type=jnp.float32)
            * scaling
        )
        value_add = jnp.einsum(
            "hqk,qhd->khd",
            probabilities.astype(jnp.bfloat16),
            grad_rows,
            preferred_element_type=jnp.float32,
        )
        return (query_add, key_add, value_add)

    def grad_block(key3, value3, k_places, k_segment):
        return grad_pair(
            query3,
            context_grad_low,
            log_total,
            delta,
            q_places,
            q_segment,
            key3,
            value3,
            k_places,
            k_segment,
        )

    zero_query = jnp.zeros((tok_rows, H, DH), jnp.float32)
    gathered_keys, gathered_values = (
        lax.all_gather(keyed, "ctx", axis=0, tiled=True),
        lax.all_gather(valued, "ctx", axis=0, tiled=True),
    )
    stream_rows = gathered_keys.shape[0]
    block_rows = math.gcd(stream_rows, 512)
    block_count = stream_rows // block_rows
    all_places, all_segment = row_places(0, stream_rows, deal_row, bounds, group_rows)

    def sweep(query_grad, pieces):
        key3, value3, block_places, block_segment = pieces
        query_add, key_add, value_add = grad_block(key3, value3, block_places, block_segment)
        return (query_grad + query_add, (key_add, value_add))

    query_grad, (key_parts, value_parts) = lax.scan(
        sweep,
        zero_query,
        (
            gathered_keys.reshape(block_count, block_rows, H, DH),
            gathered_values.reshape(block_count, block_rows, H, DH),
            all_places.reshape(block_count, block_rows),
            all_segment.reshape(block_count, block_rows),
        ),
    )
    key_terms = key_parts.reshape(stream_rows, D)
    value_terms = value_parts.reshape(stream_rows, D)
    key_grad_mine, value_grad_mine = (
        lax.psum_scatter(
            key_terms.astype(jnp.bfloat16), "ctx", scatter_dimension=0, tiled=True
        ).astype(jnp.float32),
        lax.psum_scatter(
            value_terms.astype(jnp.bfloat16), "ctx", scatter_dimension=0, tiled=True
        ).astype(jnp.float32),
    )
    qkv_grad_low = jnp.concatenate(
        [query_grad.reshape(tok_rows, D), key_grad_mine, value_grad_mine], axis=1
    ).astype(jnp.bfloat16)
    grad_qkv_w = outer_sum(normed_low, qkv_grad_low)
    column_sums = jnp.sum(qkv_grad_low.astype(jnp.float32), axis=0)
    grad_query_bias = column_sums[:D]
    grad_value_bias = column_sums[2 * D :]
    grad_normed = times_transposed(qkv_grad_low, qkv_w)
    first_pull = jax.vjp(layer_norm, inputs, gains[0], shift_rows[0])[1]
    grad_inputs_part, grad_gain_zero, grad_shift_zero = first_pull(grad_normed)
    input_grad = grad_middle + grad_inputs_part
    gains_terms = jnp.stack([grad_gain_zero, grad_gain_one, grad_gain_two])
    shift_terms = jnp.stack(
        [
            grad_shift_zero,
            grad_query_bias,
            grad_value_bias,
            grad_shift_three,
            grad_out_bias,
            grad_shift_five,
            grad_back_bias,
        ]
    )
    ffn_shift_terms = jnp.stack([grad_in_bias, grad_ffn_shift])
    reduced = (
        lax.psum_scatter(grad_qkv_w, ("ctx", "fsdp"), scatter_dimension=0, tiled=True),
        lax.psum_scatter(grad_out_w, ("ctx", "fsdp"), scatter_dimension=0, tiled=True),
        lax.psum_scatter(grad_in_w, ("ctx", "fsdp"), scatter_dimension=0, tiled=True),
        lax.psum_scatter(grad_back_w, ("ctx", "fsdp"), scatter_dimension=0, tiled=True),
        lax.psum_scatter(gains_terms, ("ctx", "fsdp"), scatter_dimension=1, tiled=True),
        lax.psum_scatter(shift_terms, ("ctx", "fsdp"), scatter_dimension=1, tiled=True),
        lax.psum_scatter(grad_ffn_gain, ("ctx", "fsdp"), scatter_dimension=0, tiled=True),
        lax.psum_scatter(ffn_shift_terms, ("ctx", "fsdp"), scatter_dimension=1, tiled=True),
    )
    return (mixed_out[None], input_grad[None]) + tuple(reduced)


def solution(mesh):
    in_specs = (
        P("fsdp", "ctx", None),
        P("fsdp", "ctx", None),
        P("fsdp", None),
        P("fsdp", None),
        P("fsdp", None),
        P("fsdp", None),
        P("fsdp", None),
        P("fsdp", None),
        P(None, "fsdp"),
        P(None, "fsdp"),
        P("fsdp"),
        P(None, "fsdp"),
    )
    out_specs = (
        P("fsdp", "ctx", None),
        P("fsdp", "ctx", None),
        P(("ctx", "fsdp"), None),
        P(("ctx", "fsdp"), None),
        P(("ctx", "fsdp"), None),
        P(("ctx", "fsdp"), None),
        P(None, ("ctx", "fsdp")),
        P(None, ("ctx", "fsdp")),
        P(("ctx", "fsdp")),
        P(None, ("ctx", "fsdp")),
    )
    return jax.shard_map(local, mesh=mesh, in_specs=in_specs, out_specs=out_specs, check_vma=False)
```

profile of v0, /device:TPU:0, one launch (start us, length us, event | category | flops | bytes accessed | tf_op | source)
XLA Modules:
  0.0 1461.8 jit_solution(8794208688010352200)
XLA Ops:
  8.0 14.9 %all-gather.1 = bf16[4,192,7]{1,2,0:T(8,128)(2,1)S(1)} all-gather(bf16[1,192,7]{1,2,0:T(8,128)(2,1)} %bitcast.267), channel_id=1, replica_groups=mesh['ctx'=8,'fsdp'=4] {'fsdp'}, dimensions={0}, use_global_device_ids=true | all-gather | bytes 13440 | tf_op jit(solution)/shard_map/all_gather | solution.py:88
  23.0 12.2 all-gather
  38.9 43.6 %all-gather.10.cloned.1.call-done = bf16[768,2304]{1,0:T(8,128)(2,1)} async-done(((bf16[192,2304]{1,0:T(8,128)(2,1)}), bf16[768,2304]{1,0:T(8,128)(2,1)}) %all-gather.10.cloned.1.call-update) | async-done | bytes 3538960 | tf_op jit(solution)/shard_map/all_gather | solution.py:83
  95.8 13.0 all_gather.45
  109.5 13.3 all-gather.2
  124.0 10.3 all-gather.12.cloned.1.call-done
  134.3 8.6 copy.91
  155.3 26.5 %all-gather.14.cloned.1.call-done = bf16[4096,768]{1,0:T(8,128)(2,1)} async-done(((bf16[512,768]{1,0:T(8,128)(2,1)}), bf16[4096,768]{1,0:T(8,128)(2,1)}) %all-gather.14.cloned.1.call-update) | async-done | bytes 6291472 | tf_op jit(solution)/shard_map/all_gather | solution.py:112
  181.8 9.3 copy.93
  202.9 179.4 %while.30 = (s32[]{:T(128)}, f32[12,512]{1,0:T(8,128)S(1)}, f32[12,512]{1,0:T(8,128)S(1)}, f32[12,512,64]{1,2,0:T(8,128)}, s32[8,512]{1,0:T(8,128)S(1)}, /*index...) while((s32[]{:T(128)}, f32[12,512]{1,0:T(8,128)S(1)}, ...), condition=%wide.region_10.11_spmd.clone, body=%wide.region_7.10_spmd.clone.sunk | while | flops 848197632 | bytes 95043760 | solution.py:141
  390.3 21.5 %fusion.101 = (f32[512]{0:T(512)S(1)}, f32[512,3072]{1,0:T(8,128)}, f32[512,3072]{1,0:T(8,128)}, f32[512,3072]{1,0:T(8,128)}) fusion(f32[3072]{0:T(1024)S(1)} %bitcast.261, bf16[768,3072]{1,0:T(8,128)(2,1)} %all-gather.18.cloned.1.call-done, f32[512,768]{1,0:T(8,128)} %copy-done.10, f32[768]{0:T(1024)S(1)} %get-tuple-element.371, ...), kind=kOutput, calls=%fused_computation.205 | convolution fusion | flops 2521693696 | bytes 25190400 | tf_op jit(solution)/shard_map/dot_general | solution.py:151
  422.6 10.6 convert_reduce_fusion
  448.0 251.3 %while.31 = (s32[]{:T(128)}, f32[512,12,64]{0,2,1:T(8,128)}, bf16[8,512,12,64]{1,3,2,0:T(8,128)(2,1)}, bf16[8,512,12,64]{1,3,2,0:T(8,128)(2,1)}, bf16[8,512,12,6...) while((s32[]{:T(128)}, f32[512,12,64]{0,2,1:T(8,128)}, ...), condition=%wide.region_24.25_spmd.clone, body=%wide.region_23.24_spmd.clone.sunk | while | flops 2047082496 | bytes 195125520 | solution.py:250
  487.0 8.4 fusion.165
  581.2 8.4 fusion.165
  612.5 8.4 fusion.165
  750.5 24.5 %reduce-scatter.14.cloned.1.call-done = bf16[512,768]{0,1:T(8,128)(2,1)} async-done(((bf16[4096,768]{0,1:T(8,128)(2,1)}), bf16[512,768]{0,1:T(8,128)(2,1)}) %reduce-scatter.14.cloned.1.call-update) | async-done | bytes 786448 | tf_op jit(solution)/shard_map/reduce_scatter | solution.py:266
  775.0 65.5 %reduce-scatter.12.cloned.1.call-done = bf16[512,768]{0,1:T(8,128)(2,1)} async-done(((bf16[4096,768]{0,1:T(8,128)(2,1)}), bf16[512,768]{0,1:T(8,128)(2,1)}) %reduce-scatter.12.cloned.1.call-update) | async-done | bytes 786448 | tf_op jit(solution)/shard_map/reduce_scatter | solution.py:263
  855.4 87.5 %reduce-scatter.24.cloned.1.call-done = f32[96,2]{1,0:T(8,128)} async-done(((f32[3072,2]{1,0:T(8,128)}), f32[96,2]{1,0:T(8,128)}) %reduce-scatter.24.cloned.1.call-update) | async-done | bytes 784
  952.8 40.7 %all-reduce.3 = (f32[3,768]{1,0:T(4,128)S(1)}, f32[7,768]{1,0:T(8,128)S(1)}, f32[3072]{0:T(1024)S(1)}) all-reduce(f32[3,768]{1,0:T(4,128)S(1)} %pad_maximum_fusion.2, f32[7,768]{1,0:T(8,128)S(1)} %stack.36, f32[3072]{0:T(1024)S(1)} %copy-done.25), channel_id=8, replica_groups=mesh['ctx'=8,'fsdp'=4] {'ctx','fsdp'}, use_global_device_ids=true, to_apply=%region_36.37.clone | all-reduce | flops 10752 | bytes 86016
  995.4 51.3 %reduce-scatter.18.cloned.1.call-done = f32[24,768]{1,0:T(8,128)} async-done(((f32[768,768]{1,0:T(8,128)}), f32[24,768]{1,0:T(8,128)}) %reduce-scatter.18.cloned.1.call-update) | async-done | bytes 73744 | tf_op jit(solution)/shard_map/reduce_scatter | solution.py:296
  1046.7 142.0 %reduce-scatter.20.cloned.1.call-done = f32[24,3072]{1,0:T(8,128)} async-done(((f32[768,3072]{1,0:T(8,128)}), f32[24,3072]{1,0:T(8,128)}) %reduce-scatter.20.cloned.1.call-update) | async-done | bytes 294928 | tf_op jit(solution)/shard_map/reduce_scatter | solution.py:297
  1188.6 140.9 %reduce-scatter.22.cloned.1.call-done = f32[96,768]{1,0:T(8,128)} async-done(((f32[3072,768]{1,0:T(8,128)}), f32[96,768]{1,0:T(8,128)}) %reduce-scatter.22.cloned.1.call-update) | async-done | bytes 294928 | tf_op jit(solution)/shard_map/reduce_scatter | solution.py:298
  1329.5 125.5 %reduce-scatter.16.cloned.1.call-done = f32[24,2304]{1,0:T(8,128)} async-done(((f32[768,2304]{1,0:T(8,128)}), f32[24,2304]{1,0:T(8,128)}) %reduce-scatter.16.cloned.1.call-update) | async-done | bytes 221200 | tf_op jit(solution)/shard_map/reduce_scatter | solution.py:295
  (411 shorter events, 558.3 us)
Async XLA Ops:
  7.2 75.3 %all-gather.10.cloned.1.call-start = ((), (), s32[]{:S(2)}) async-start(), calls=%async_computation.7 | async-start | bytes 4423680 | tf_op jit(solution)/shard_map/all_gather | solution.py:83
  7.9 126.4 %all-gather.12.cloned.1.call-start = ((), (), s32[]{:S(2)}) async-start(), calls=%async_computation.8 | async-start | bytes 7077888 | tf_op jit(solution)/shard_map/all_gather | solution.py:111
  35.4 51.5 %copy-start.26 = (f32[768]{0:T(1024)}, f32[768]{0:T(1024)S(1)}, u32[]{:S(2)}) copy-start(f32[768]{0:T(1024)S(1)} %get-tuple-element.379) | copy-start | bytes 9220
  36.0 50.9 %copy-start.39 = (f32[768]{0:T(1024)}, f32[768]{0:T(1024)S(1)}, u32[]{:S(2)}) copy-start(f32[768]{0:T(1024)S(1)} %get-tuple-element.376) | copy-start | bytes 9220
  36.0 350.0 %copy-start.43 = (f32[768]{0:T(1024)}, f32[768]{0:T(1024)S(1)}, u32[]{:S(2)}) copy-start(f32[768]{0:T(1024)S(1)} %get-tuple-element.373) | copy-start | bytes 9220
  36.0 354.3 %copy-start.41 = (f32[768]{0:T(1024)}, f32[768]{0:T(1024)S(1)}, u32[]{:S(2)}) copy-start(f32[768]{0:T(1024)S(1)} %get-tuple-element.371) | copy-start | bytes 9220
  37.3 49.5 %copy-start.28 = (f32[512]{0:T(512)}, f32[512]{0:T(512)S(1)}, u32[]{:S(2)}) copy-start(f32[512]{0:T(512)S(1)} %broadcast_multiply_fusion.4) | copy-start | bytes 6148
  38.8 48.0 %copy-start.32 = (f32[512]{0:T(512)}, f32[512]{0:T(512)S(1)}, u32[]{:S(2)}) copy-start(f32[512]{0:T(512)S(1)} %fusion.57) | copy-start | bytes 6148
  90.1 91.7 %all-gather.14.cloned.1.call-start = ((), (), s32[]{:S(2)}) async-start(), calls=%async_computation.9 | async-start | bytes 7077888 | tf_op jit(solution)/shard_map/all_gather | solution.py:112
  93.2 292.7 %all-gather.16.cloned.1.call-start = ((), (), s32[]{:S(2)}) async-start(), calls=%async_computation.10 | async-start | bytes 1474560 | tf_op jit(solution)/shard_map/all_gather | solution.py:84
  93.8 296.5 %all-gather.18.cloned.1.call-start = ((), (), s32[]{:S(2)}) async-start(), calls=%async_computation.11 | async-start | bytes 5898240 | tf_op jit(solution)/shard_map/all_gather | solution.py:85
  94.4 317.4 %all-gather.20.cloned.1.call-start = ((), (), s32[]{:S(2)}) async-start(), calls=%async_computation.12 | async-start | bytes 5898240 | tf_op jit(solution)/shard_map/all_gather | solution.py:86
  94.9 680.0 %reduce-scatter.14.cloned.1.call-start = ((), (), s32[]{:S(2)}) async-start(), calls=%async_computation.14 | async-start | bytes 7077888 | tf_op jit(solution)/shard_map/reduce_scatter | solution.py:266
  713.0 127.5 %reduce-scatter.12.cloned.1.call-start = ((), (), s32[]{:S(2)}) async-start(), calls=%async_computation.13 | async-start | bytes 7077888 | tf_op jit(solution)/shard_map/reduce_scatter | solution.py:263
  727.3 215.5 %reduce-scatter.24.cloned.1.call-start = ((), (), s32[]{:S(2)}) async-start(), calls=%async_computation.19 | async-start | bytes 1622016
  729.8 316.9 %reduce-scatter.18.cloned.1.call-start = ((), (), s32[]{:S(2)}) async-start(), calls=%async_computation.16 | async-start | bytes 2433024 | tf_op jit(solution)/shard_map/reduce_scatter | solution.py:296
  733.5 455.1 %reduce-scatter.20.cloned.1.call-start = ((), (), s32[]{:S(2)}) async-start(), calls=%async_computation.17 | async-start | bytes 9732096 | tf_op jit(solution)/shard_map/reduce_scatter | solution.py:297
  740.8 588.7 %reduce-scatter.22.cloned.1.call-start = ((), (), s32[]{:S(2)}) async-start(), calls=%async_computation.18 | async-start | bytes 9732096 | tf_op jit(solution)/shard_map/reduce_scatter | solution.py:298
  748.9 91.6 %copy-start.9 = (bf16[1,512,768]{2,1,0:T(8,128)(2,1)S(1)}, bf16[1,512,768]{2,1,0:T(8,128)(2,1)}, u32[]{:S(2)}) copy-start(bf16[1,512,768]{2,1,0:T(8,128)(2,1)} %param.16) | copy-start | bytes 2359300
  748.9 91.6 %copy-start.27 = (f32[768]{0:T(1024)S(1)}, f32[768]{0:T(1024)}, u32[]{:S(2)}) copy-start(f32[768]{0:T(1024)} %copy-done.26) | copy-start | bytes 9220
  748.9 91.6 %copy-start.29 = (f32[512]{0:T(512)S(1)}, f32[512]{0:T(512)}, u32[]{:S(2)}) copy-start(f32[512]{0:T(512)} %copy-done.28) | copy-start | bytes 6148
  748.9 91.6 %copy-start.31 = (f32[512]{0:T(512)S(1)}, f32[512]{0:T(512)}, u32[]{:S(2)}) copy-start(f32[512]{0:T(512)} %copy-done.30) | copy-start | bytes 6148
  748.9 91.6 %copy-start.40 = (f32[768]{0:T(1024)S(1)}, f32[768]{0:T(1024)}, u32[]{:S(2)}) copy-start(f32[768]{0:T(1024)} %copy-done.39) | copy-start | bytes 9220
  749.0 706.0 %reduce-scatter.16.cloned.1.call-start = ((), (), s32[]{:S(2)}) async-start(), calls=%async_computation.15 | async-start | bytes 7299072 | tf_op jit(solution)/shard_map/reduce_scatter | solution.py:295
  (71 other events, 431.5 us)
Sparse Core Ops, SparseCore 0:
  9.6 72.8 all-gather.9
  90.2 44.0 all-gather.11
  136.2 45.5 all-gather.13
  183.2 30.4 all-gather.15
  215.1 88.5 all-gather.17
  305.1 87.8 all-gather.19
  713.1 61.7 reduce-scatter.13
  778.7 61.7 reduce-scatter.11
  845.7 97.0 reduce-scatter.23
  948.6 98.0 reduce-scatter.17
  1054.1 134.4 reduce-scatter.19
  1195.0 134.5 reduce-scatter.21
  1336.7 118.2 reduce-scatter.15
where the time goes:
time: 1470 us; the launch traced here: 1460 us
  waiting for transfers between devices  720 us (49%)
  matrix products  403 us (27%)
  local copies, waits for them, and re-layouts  131 us (9%)
  other arithmetic  95.9 us (7%)
  blocking collectives  94.2 us (6%)
  between operations  14.9 us (1%)
    reduce_scatter x1, waiting for transfers between devices, local(): lax.psum_scatter(grad_in_w, ('ctx', 'fsdp'), scatter_dimension=0, tiled=T...  142 us
    reduce_scatter x1, waiting for transfers between devices, local(): lax.psum_scatter(grad_back_w, ('ctx', 'fsdp'), scatter_dimension=0, tiled...  141 us
    reduce_scatter x1, waiting for transfers between devices, local(): lax.psum_scatter(grad_qkv_w, ('ctx', 'fsdp'), scatter_dimension=0, tiled=...  125 us
    unnamed x14, waiting for transfers between devices  89.9 us
    dot_general x8, matrix products, grad_pair(): jnp.einsum('qhd,khd->hqk', grad_rows, value3, preferred_element_type=jnp....  67.5 us
    reduce_scatter x1, waiting for transfers between devices, local(): lax.psum_scatter(key_terms.astype(jnp.bfloat16), 'ctx', scatter_dimension...  65.5 us
    dot_general x8, matrix products, visit_block(): jnp.einsum('qhd,khd->hqk', query3, key3, preferred_element_type=jnp.float32)  64 us
    reduce_sum x8, other arithmetic, visit_block(): totals = totals * rescale + jnp.sum(expo, axis=-1)  61.3 us
  transfers between devices with their start and end apart: 13, of which 10 were waited for; matrix products, arithmetic and copies ran while one was open for 21% of the time, Pallas kernels for 0%

commit v1 on v0

v1 whole, which is shorter than its diff:
```python
import functools

import jax
import jax.numpy as jnp
from jax import lax
from jax.experimental import pallas as pl
from jax.experimental.pallas import tpu as pltpu
from jax.sharding import PartitionSpec as P

D = 768
H = 12
DH = 64
FF = 3072
GROUP = 256
HPG = 3
TP = H // HPG
HC = HPG * DH
LANES = 256
SCALE2 = 1.4426950408889634 * DH ** -0.5
NEG = -1e30
NT = (((1,), (1,)), ((), ()))
F32 = jnp.float32
BF16 = jnp.bfloat16

SMEM = pltpu.MemorySpace.SMEM
VM = pltpu.MemorySpace.VMEM
HW = 2 * DH
WIDE = HPG * HW


def cost(us):
    return pl.CostEstimate(flops=int(us * 1.1e9), transcendentals=0, bytes_accessed=100000)


def block_bounds(group, bound_ref):
    lane = lax.broadcasted_iota(jnp.int32, (1, GROUP), 1)
    q_places = group * GROUP + lane
    starts = jnp.zeros((1, GROUP), jnp.int32)
    first = jnp.int32(0)
    last = jnp.int32(0)
    for j in range(bound_ref.shape[0]):
        b = bound_ref[j]
        starts = jnp.where(q_places >= b, b, starts)
        first = jnp.where(group * GROUP >= b, b, first)
        last = jnp.where(group * GROUP + GROUP - 1 >= b, b, last)
    low = first // GROUP
    mid = jnp.minimum(group, (last + GROUP - 1) // GROUP)
    return q_places, starts, low, mid


def sweep(group, low, mid, visit):
    lax.fori_loop(mid, group, lambda kg, c: visit(kg, False), None)

    def edge(t, c):
        kg = jnp.where(low + t < mid, low + t, group)
        return visit(kg, True)

    lax.fori_loop(0, mid - low + 1, edge, None)


def allowed_pairs(kg, q_places, starts):
    k_places = kg * GROUP + lax.broadcasted_iota(jnp.int32, (GROUP, 1), 0)
    return (k_places <= q_places) & (k_places >= starts)


def group_rows(index):
    return pl.ds(pl.multiple_of(index * GROUP, GROUP), GROUP)


def project_kernel(count, *refs):
    tok_refs = refs[:count]
    w_ref, row_ref, bias_ref, a_ref, q_ref, kv_ref = refs[count:]
    at = 0
    for ref in tok_refs:

        def part(i, c, ref=ref, at=at):
            rows = pl.ds(pl.multiple_of(i * GROUP, GROUP), GROUP)
            to = pl.ds(pl.multiple_of(at + i * GROUP, GROUP), GROUP)
            value = ref[rows, :].astype(F32)
            centred = value - jnp.mean(value, axis=1, keepdims=True)
            variance = jnp.mean(centred * centred, axis=1, keepdims=True)
            normed = centred * lax.rsqrt(variance + 1e-05) * row_ref[0:1, :] + row_ref[1:2, :]
            normed = normed.astype(BF16)
            a_ref[to, :] = normed
            out = jnp.dot(normed, w_ref[...], preferred_element_type=F32) + bias_ref[0:1, :]
            kv_ref[to, :] = out[:, :WIDE].astype(BF16)
            none = jnp.zeros((GROUP, DH), BF16)
            heads = []
            for h in range(HPG):
                lane = WIDE + h * DH
                heads += [out[:, lane : lane + DH].astype(BF16), none]
            q_ref[to, :] = jnp.concatenate(heads, axis=1)
            return c

        lax.fori_loop(0, ref.shape[0] // GROUP, part, None)
        at += ref.shape[0]


def project(toks, weight, norm_rows, bias):
    n = sum(t.shape[0] for t in toks)
    return pl.pallas_call(
        functools.partial(project_kernel, len(toks)),
        name="project",
        in_specs=[pl.BlockSpec(memory_space=VM)] * (len(toks) + 3),
        out_specs=[pl.BlockSpec(memory_space=VM)] * 3,
        out_shape=[
            jax.ShapeDtypeStruct((n, D), BF16),
            jax.ShapeDtypeStruct((n, WIDE), BF16),
            jax.ShapeDtypeStruct((n, WIDE), BF16),
        ],
        cost_estimate=cost(4 + n // 512),
    )(*toks, weight, norm_rows, bias)


def forward_kernel(chunks, key_chunks, *refs):
    dealt_ref, bound_ref = refs[:2]
    q_refs = refs[2 : 2 + chunks]
    kv_refs = refs[2 + chunks : 2 + chunks + key_chunks]
    o_refs = refs[2 + chunks + key_chunks : 2 + chunks + key_chunks + TP]
    ot_ref, lse_ref, qt_ref, kv_ref, kvt_ref, o_ref, acc_ref = refs[
        2 + chunks + key_chunks + TP :
    ]
    at = 0
    for ref in kv_refs:
        for j in range(ref.shape[0] // GROUP):
            rows = group_rows(dealt_ref[at])
            block = ref[j * GROUP : (j + 1) * GROUP, :]
            kv_ref[rows, :] = block
            kvt_ref[:, rows] = block.T
            at += 1
    at = 0
    for ref in q_refs:
        for j in range(ref.shape[0] // GROUP):
            qt_ref[:, at * GROUP : (at + 1) * GROUP] = ref[j * GROUP : (j + 1) * GROUP, :].T
            at += 1

    def one(i, c):
        group = dealt_ref[i]
        rows = group_rows(i)
        q_places, starts, low, mid = block_bounds(group, bound_ref)
        acc_ref[...] = jnp.zeros_like(acc_ref)

        def visit(kg, masked, carry):
            cols = group_rows(kg)
            allowed = allowed_pairs(kg, q_places, starts) if masked else None
            out = []
            for h in range(HPG):
                lanes = slice(h * HW, (h + 1) * HW)
                s = jnp.dot(kv_ref[cols, lanes], qt_ref[lanes, rows], preferred_element_type=F32)
                if masked:
                    s = jnp.where(allowed, s, NEG)
                old, total = carry[h]
                new = jnp.maximum(old, jnp.max(s, axis=0, keepdims=True))
                p = jnp.exp2((s - new) * SCALE2)
                alpha = jnp.exp2((old - new) * SCALE2)
                total = total * alpha + jnp.sum(p, axis=0, keepdims=True)
                part = slice(h * DH, (h + 1) * DH)
                acc_ref[part, :] = acc_ref[part, :] * alpha + jnp.dot(
                    kvt_ref[h * HW + DH : (h + 1) * HW, cols],
                    p.astype(BF16),
                    preferred_element_type=F32,
                )
                out.append((new, total))
            return tuple(out)

        start = tuple(
            (jnp.full((1, GROUP), NEG, F32), jnp.zeros((1, GROUP), F32)) for _ in range(HPG)
        )
        carry = lax.fori_loop(mid, group, lambda kg, c: visit(kg, False, c), start)

        def edge(t, c):
            return visit(jnp.where(low + t < mid, low + t, group), True, c)

        carry = lax.fori_loop(0, mid - low + 1, edge, carry)
        for h in range(HPG):
            part = slice(h * DH, (h + 1) * DH)
            acc_ref[part, :] = acc_ref[part, :] / carry[h][1]
            lse_ref[h : h + 1, rows] = carry[h][0] * SCALE2 + jnp.log2(carry[h][1])
        ot_ref[:, rows] = acc_ref[0:HC, :]
        o_ref[rows, :] = acc_ref[...].T.astype(BF16)
        return c

    lax.fori_loop(0, o_ref.shape[0] // GROUP, one, None)
    for m, ref in enumerate(o_refs):
        half = ref.shape[0]
        low = o_ref[2 * m * half : (2 * m + 1) * half, :HC]
        high = o_ref[(2 * m + 1) * half : (2 * m + 2) * half, :HC]
        ref[...] = jnp.concatenate([low, high], axis=1)


def attend_forward(dealt, bounds, queries, pairs):
    n = sum(q.shape[0] for q in queries)
    s = sum(p.shape[0] for p in pairs)
    return pl.pallas_call(
        functools.partial(forward_kernel, len(queries), len(pairs)),
        name="attend_forward",
        in_specs=[pl.BlockSpec(memory_space=SMEM)] * 2
        + [pl.BlockSpec(memory_space=VM)] * (len(queries) + len(pairs)),
        out_specs=[pl.BlockSpec(memory_space=VM)] * (TP + 5),
        out_shape=[jax.ShapeDtypeStruct((n // TP // 2, 2 * HC), BF16)] * TP
        + [
            jax.ShapeDtypeStruct((HC, n), F32),
            jax.ShapeDtypeStruct((8, n), F32),
            jax.ShapeDtypeStruct((WIDE, n), BF16),
            jax.ShapeDtypeStruct((s, WIDE), BF16),
            jax.ShapeDtypeStruct((WIDE, s), BF16),
        ],
        scratch_shapes=[
            pltpu.VMEM((n, LANES), BF16),
            pltpu.VMEM((LANES, GROUP), F32),
        ],
        cost_estimate=cost(36),
    )(dealt, bounds, *queries, *pairs)


def backward_kernel(h, dealt_ref, bound_ref, qt_ref, kv_ref, kt_ref, ot_ref, lse_ref, *refs):
    do_refs = refs[:TP]
    dq_ref, own_ref, other_ref, qd_ref, qdt_ref, acc_ref, sum_ref = refs[TP:]
    n = dq_ref.shape[0]
    sum_ref[...] = jnp.zeros_like(sum_ref)
    qd_ref[...] = jnp.zeros_like(qd_ref)
    qdt_ref[...] = jnp.zeros_like(qdt_ref)
    half = do_refs[0].shape[0]
    for m, ref in enumerate(do_refs):
        for j in range(2):
            block = ref[:, j * HC + h * DH : j * HC + (h + 1) * DH]
            part = slice((2 * m + j) * half, (2 * m + j + 1) * half)
            qd_ref[1, part, DH:] = block
            qdt_ref[1, DH:, part] = block.T
    qdt_ref[0] = qt_ref[...]

    def turn(i, c):
        rows = group_rows(i)
        qd_ref[0, rows, :] = qt_ref[:, rows].T
        return c

    lax.fori_loop(0, n // GROUP, turn, None)

    def one(i, c):
        group = dealt_ref[i]
        rows = group_rows(i)
        q_places, starts, low, mid = block_bounds(group, bound_ref)
        delta = jnp.sum(qdt_ref[1, DH:, rows].astype(F32) * ot_ref[:, rows], axis=0, keepdims=True)
        lse = lse_ref[h : h + 1, rows]
        acc_ref[...] = jnp.zeros_like(acc_ref)

        def visit(kg, masked):
            cols = group_rows(kg)
            kv = kv_ref[cols, :]
            s = jnp.dot(kv, qdt_ref[0, :, rows], preferred_element_type=F32)
            dp = jnp.dot(kv, qdt_ref[1, :, rows], preferred_element_type=F32)
            if masked:
                s = jnp.where(allowed_pairs(kg, q_places, starts), s, NEG)
            p = jnp.exp2(s * SCALE2 - lse)
            d = (p * (dp - delta)).astype(BF16)
            acc_ref[...] += jnp.dot(kt_ref[0:DH, cols], d, preferred_element_type=F32)
            sum_ref[cols, :] += jnp.dot(
                d, qd_ref[0, rows, :], preferred_element_type=F32
            ) + jnp.dot(p.astype(BF16), qd_ref[1, rows, :], preferred_element_type=F32)

        sweep(group, low, mid, visit)
        dq_ref[rows, :] = (acc_ref[...] * DH**-0.5).T.astype(BF16)
        return c

    lax.fori_loop(0, n // GROUP, one, None)
    lane = lax.broadcasted_iota(jnp.int32, (1, HW), 1)
    scale = jnp.where(lane < DH, DH**-0.5, 1.0)

    def store(b, c):
        own_ref[group_rows(b), :] = sum_ref[group_rows(dealt_ref[b]), :] * scale
        return c

    lax.fori_loop(0, n // GROUP, store, None)

    def other(b, c):
        source = group_rows(dealt_ref[n // GROUP + b])
        other_ref[group_rows(b), :] = (sum_ref[source, :] * scale).astype(BF16)
        return c

    lax.fori_loop(0, other_ref.shape[0] // GROUP, other, None)


def attend_backward(h, dealt, bounds, qt, kv, kvt, ot, lse, grads):
    n = ot.shape[1]
    s = kv.shape[0]
    full = pl.BlockSpec(memory_space=VM)
    return pl.pallas_call(
        functools.partial(backward_kernel, h),
        name="attend_backward",
        grid=(1,),
        in_specs=[pl.BlockSpec(memory_space=SMEM)] * 2
        + [
            pl.BlockSpec((HW, n), lambda i: (h, 0)),
            pl.BlockSpec((s, HW), lambda i: (0, h)),
            pl.BlockSpec((HW, s), lambda i: (h, 0)),
            pl.BlockSpec((DH, n), lambda i: (h, 0)),
            full,
        ]
        + [full] * TP,
        out_specs=[full] * 3,
        out_shape=[
            jax.ShapeDtypeStruct((n, DH), BF16),
            jax.ShapeDtypeStruct((n, HW), F32),
            jax.ShapeDtypeStruct((s - n, HW), BF16),
        ],
        scratch_shapes=[
            pltpu.VMEM((2, n, HW), BF16),
            pltpu.VMEM((2, HW, n), BF16),
            pltpu.VMEM((DH, GROUP), F32),
            pltpu.VMEM((s, HW), F32),
        ],
        cost_estimate=cost(19),
    )(dealt, bounds, qt, kv, kvt, ot, lse, *grads)


def finish_kernel(shifts, *refs):
    dq_refs = refs[:HPG]
    own_refs = refs[HPG : 2 * HPG]
    came_refs = refs[2 * HPG : (2 + shifts) * HPG]
    outs = refs[(2 + shifts) * HPG :]
    sums_ref = outs[TP]
    sums_ref[...] = jnp.zeros_like(sums_ref)
    size = outs[0].shape[0]
    for m in range(TP):

        def part(i, c, m=m):
            to = pl.ds(pl.multiple_of(i * 128, 128), 128)
            rows = pl.ds(pl.multiple_of(m * size + i * 128, 128), 128)
            pieces = []
            for h in range(HPG):
                value = own_refs[h][rows, :]
                for s in range(shifts):
                    value = value + came_refs[s * HPG + h][rows, :].astype(F32)
                pieces.append(value.astype(BF16))
            for h in range(HPG):
                pieces.append(dq_refs[h][rows, :])
            whole = jnp.concatenate(pieces, axis=1)
            outs[m][to, :] = whole
            sums_ref[0:1, :] += jnp.sum(whole.astype(F32), axis=0, keepdims=True)
            return c

        lax.fori_loop(0, size // 128, part, None)


def finish(dqs, owns, cames):
    n = dqs[0].shape[0]
    full = pl.BlockSpec(memory_space=VM)
    shifts = len(cames) // HPG
    return pl.pallas_call(
        functools.partial(finish_kernel, shifts),
        name="finish",
        in_specs=[full] * ((2 + shifts) * HPG),
        out_specs=[full] * (TP + 1),
        out_shape=[jax.ShapeDtypeStruct((n // TP, 3 * HC), BF16)] * TP
        + [jax.ShapeDtypeStruct((8, 3 * HC), F32)],
        cost_estimate=cost(6),
    )(*dqs, *owns, *cames)


TN = (((0,), (0,)), ((), ()))


def columns_kernel(chunks, place_ref, *refs):
    a_refs = refs[:chunks]
    g_refs = refs[chunks : chunks + TP]
    w_ref, sums_ref, norm_ref, extra_ref = refs[chunks + TP : chunks + TP + 4]
    keep_ref, send_ref, out_ref = refs[chunks + TP + 4 :]
    width = 3 * HC
    at = 0
    size = g_refs[0].shape[0]
    spans = []
    for ref in a_refs:
        for first in range(0, ref.shape[0], size):
            spans.append((ref, first))
    for m, (ref, first) in enumerate(spans):
        value = lax.dot_general(
            ref[first : first + size, :], g_refs[m][...], TN, preferred_element_type=F32
        )
        if m:
            out_ref[:, :width] += value
        else:
            out_ref[:, :width] = value
    sums = sums_ref[0:1, :]
    weight = w_ref[...].astype(F32)
    lane = lax.broadcasted_iota(jnp.int32, (1, 64), 1)
    plain = (out_ref[:, :width] - norm_ref[:, 1:2] * sums) / norm_ref[:, 0:1]
    gain = jnp.sum(plain * weight, axis=1, keepdims=True)
    shift = jnp.sum(weight * sums, axis=1, keepdims=True)
    out_ref[:, width:] = (
        extra_ref[...] + jnp.where(lane == 0, gain, 0.0) + jnp.where(lane == 1, shift, 0.0)
    )
    turned = sums_ref[...].T
    query = turned[WIDE:, 0:1]
    value = jnp.concatenate(
        [turned[h * HW + DH : (h + 1) * HW, 0:1] for h in range(HPG)], axis=0
    )
    own = pl.ds(pl.multiple_of(place_ref[0] * HC, HC), HC)
    out_ref[own, width:] += jnp.where(lane == 4, query, 0.0) + jnp.where(lane == 5, value, 0.0)
    half = HC // 2
    for g in range(TP):
        mine = pl.multiple_of(g * HC + place_ref[1] * half, half)
        other = pl.multiple_of(g * HC + (1 - place_ref[1]) * half, half)
        keep_ref[g] = out_ref[pl.ds(mine, half), :]
        send_ref[g] = out_ref[pl.ds(other, half), :]


def columns(place, normed, grads, weight, sums, norm_columns, extra):
    full = pl.BlockSpec(memory_space=VM)
    out = jax.ShapeDtypeStruct((TP, HC // 2, 3 * HC + 64), F32)
    return pl.pallas_call(
        functools.partial(columns_kernel, len(normed)),
        name="columns",
        in_specs=[pl.BlockSpec(memory_space=SMEM)] + [full] * (len(normed) + TP + 4),
        out_specs=[full] * 2,
        out_shape=[out, out],
        scratch_shapes=[pltpu.VMEM((D, 3 * HC + 64), F32)],
        cost_estimate=cost(8),
    )(place, *normed, *grads, weight, sums, norm_columns, extra)


def weight_grads_kernel(
    place_ref,
    u_ref,
    datt_ref,
    a2_ref,
    df_ref,
    u2_ref,
    dz_ref,
    keep_ref,
    send_ref,
    back_ref,
    in_ref,
    out_ref,
    sems,
):
    hg = place_ref[0]
    qs = place_ref[1]

    def each(source, k, rows, sem, act):
        block = (k // 2) ^ hg
        to = pl.ds(rows, source.shape[0])
        kept = k % 2 == qs
        pl.when(kept)(lambda: act(pltpu.make_async_copy(source, keep_ref.at[block, to], sem)))
        pl.when(jnp.logical_not(kept))(
            lambda: act(pltpu.make_async_copy(source, send_ref.at[block, to], sem))
        )

    def start(source, k, rows, sem):
        each(source, k, rows, sem, lambda copy: copy.start())

    def wait(source, k, rows, sem):
        each(source, k, rows, sem, lambda copy: copy.wait())

    def back_block(k):
        return back_ref.at[pl.ds(pl.multiple_of(k * 384, 384), 384)]

    def in_block(k, j):
        return in_ref.at[j, pl.ds(pl.multiple_of(k * 96, 96), 96)]

    def out_block(k):
        at = ((k // 2) ^ hg) * 192 + (k % 2) * 96
        return out_ref.at[pl.ds(pl.multiple_of(at, 96), 96)]

    def back(k, c):
        lanes = pl.ds(pl.multiple_of(k * 384, 384), 384)
        back_ref[pl.ds(pl.multiple_of(k * 384, 384), 384), :] = lax.dot_general(
            u2_ref[:, lanes], dz_ref[...], TN, preferred_element_type=F32
        ).astype(BF16)
        start(back_block(k), k, 0, sems.at[0, k])
        return c

    lax.fori_loop(0, 8, back, None)

    def inner(j, c):
        lanes = pl.ds(pl.multiple_of(j * D, D), D)
        in_ref[j] = lax.dot_general(
            a2_ref[...], df_ref[:, lanes], TN, preferred_element_type=F32
        ).astype(BF16)
        return c

    lax.fori_loop(0, 4, inner, None)

    def send_inner(k, c):
        for j in range(4):
            start(in_block(k, j), k, 384 + 96 * j, sems.at[1 + j, k])
        return c

    lax.fori_loop(0, 8, send_inner, None)
    out_ref[...] = lax.dot_general(
        u_ref[...], datt_ref[...], TN, preferred_element_type=F32
    ).astype(BF16)

    def finish_all(k, c):
        start(out_block(k), k, 768, sems.at[5, k])
        wait(back_block(k), k, 0, sems.at[0, k])
        for j in range(4):
            wait(in_block(k, j), k, 384 + 96 * j, sems.at[1 + j, k])
        return c

    lax.fori_loop(0, 8, finish_all, None)

    def finish_out(k, c):
        wait(out_block(k), k, 768, sems.at[5, k])
        return c

    lax.fori_loop(0, 8, finish_out, None)


def weight_grads(place, u, datt, a2, df, u2, dz):
    full = pl.BlockSpec(memory_space=VM)
    out = jax.ShapeDtypeStruct((TP, 864, D), BF16)
    return pl.pallas_call(
        weight_grads_kernel,
        name="weight_grads",
        in_specs=[pl.BlockSpec(memory_space=SMEM)] + [full] * 6,
        out_specs=[pl.BlockSpec(memory_space=pl.ANY)] * 2,
        out_shape=[out, out],
        scratch_shapes=[
            pltpu.VMEM((FF, D), BF16),
            pltpu.VMEM((4, D, D), BF16),
            pltpu.VMEM((D, D), BF16),
            pltpu.SemaphoreType.DMA((6, 8)),
        ],
        cost_estimate=cost(14),
    )(place, u, datt, a2, df, u2, dz)


def norm_parts(value):
    centred = value - jnp.mean(value, axis=1, keepdims=True)
    scale = lax.rsqrt(jnp.mean(centred * centred, axis=1, keepdims=True) + 1e-05)
    return centred * scale, scale


def norm_back(grad, unit, scale):
    first = jnp.mean(grad, axis=1, keepdims=True)
    second = jnp.mean(grad * unit, axis=1, keepdims=True)
    return scale * (grad - first - unit * second)


def column_sum(value):
    return jnp.sum(value, axis=0, keepdims=True)


CHUNK = 768
TILE = 256


def place_weights(place_ref, own_refs, gathered, in_ref, out_ref, back_ref):
    near, axis, axis_far, corner, corner_far = gathered
    in_ref[pl.ds(pl.multiple_of(place_ref[0] * 192, 192), 192), :] = own_refs[0][...]
    out_ref[pl.ds(pl.multiple_of(place_ref[4] * 192, 192), 192), :] = own_refs[1][...]
    back_ref[pl.ds(pl.multiple_of(place_ref[0] * D, D), D), :] = own_refs[2][...]
    sources = [
        (near, 0),
        (near, 1),
        (axis, 0),
        (axis, 1),
        (axis_far, 0),
        (axis_far, 1),
        (corner, None),
        (corner_far, None),
    ]
    for k, (ref, t) in enumerate(sources):
        c = place_ref[8 + k]
        for m in range(1, 4):
            value = ref[m - 1] if t is None else ref[t, m - 1]
            z = place_ref[m]
            cols = pl.ds(pl.multiple_of(c * 384, 384), 384)
            in_ref[pl.ds(pl.multiple_of(z * 192, 96), 96), cols] = value[0:96, 0:384]
            in_ref[pl.ds(pl.multiple_of(z * 192 + 96, 96), 96), cols] = value[0:96, 384:768]
            back_ref[pl.ds(pl.multiple_of(z * D + c * 96, 96), 96), :] = value[96:192, :]
            block = jnp.concatenate([value[192:216, 0:384], value[192:216, 384:768]], axis=0)
            at = pl.ds(pl.multiple_of(place_ref[4 + m] * 192 + (c // 2) * 48, 48), 48)
            out_ref[at, pl.ds(pl.multiple_of((c % 2) * 384, 384), 384)] = block


def middle_kernel(scattered, *refs):
    piece_refs = refs[:TP]
    x_ref, cot_ref, row_ref, wide_ref = refs[TP : TP + 4]
    refs = refs[TP + 4 :]
    if scattered:
        place_ref = refs[0]
        own_refs, gathered, refs = refs[1:4], refs[4:9], refs[9:]
        out_w_ref, in_w_ref, back_w_ref = refs[-3:]
        place_weights(place_ref, own_refs, gathered, in_w_ref, out_w_ref, back_w_ref)
        refs = refs[:-3]
    else:
        in_w_ref, out_w_ref, back_w_ref = refs[:3]
        refs = refs[3:]
    do_refs = refs[:TP]
    (
        mixed_ref,
        u_ref,
        a2_ref,
        u2_ref,
        df_ref,
        datt_ref,
        dx_ref,
        narrow_ref,
        broad_ref,
        ctx_ref,
        do_ref,
        g_ref,
        slope_ref,
        d_ref,
        da_ref,
        x1_ref,
    ) = refs[TP:]
    half = piece_refs[0].shape[0]
    for m, ref in enumerate(piece_refs):
        for j in range(2):
            ctx_ref[j * half : (j + 1) * half, m * HC : (m + 1) * HC] = ref[
                :, j * HC : (j + 1) * HC
            ]
    narrow_ref[...] = jnp.zeros_like(narrow_ref)
    broad_ref[...] = jnp.zeros_like(broad_ref)

    def tile(i, c):
        rows = pl.ds(pl.multiple_of(i * TILE, TILE), TILE)
        unit_one, scale_one = norm_parts(ctx_ref[rows, :].astype(F32))
        u = (unit_one * row_ref[0:1, :] + row_ref[1:2, :]).astype(BF16)
        u_ref[rows, :] = u
        x1 = (
            x_ref[rows, :].astype(F32)
            + jnp.dot(u, out_w_ref[...], preferred_element_type=F32)
            + row_ref[2:3, :]
        )
        x1_ref[...] = x1
        unit_two, scale_two = norm_parts(x1)
        a2 = (unit_two * row_ref[3:4, :] + row_ref[4:5, :]).astype(BF16)
        a2_ref[rows, :] = a2

        def lanes_of(j):
            return pl.ds(pl.multiple_of(j * CHUNK, CHUNK), CHUNK)

        def up(j, total):
            lanes = lanes_of(j)
            f = (
                jnp.dot(a2_ref[rows, :], in_w_ref[:, lanes], preferred_element_type=F32)
                + wide_ref[0:1, lanes]
            )
            cdf = 0.5 * (1.0 + lax.erf(f * 0.7071067811865476))
            pdf = jnp.exp(-0.5 * f * f) * 0.3989422804014327
            slope_ref[:, lanes] = cdf + f * pdf
            g = f * cdf
            g_ref[:, lanes] = g
            return total + jnp.sum(g, axis=1, keepdims=True)

        average = lax.fori_loop(0, FF // CHUNK, up, jnp.zeros((TILE, 1), F32)) / FF

        def spread(j, total):
            lanes = lanes_of(j)
            centred = g_ref[:, lanes] - average
            return total + jnp.sum(centred * centred, axis=1, keepdims=True)

        variance = lax.fori_loop(0, FF // CHUNK, spread, jnp.zeros((TILE, 1), F32)) / FF
        scale = lax.rsqrt(variance + 1e-05)

        def turn(j, carry):
            first, second = carry
            lanes = lanes_of(j)
            unit = (g_ref[:, lanes] - average) * scale
            g_ref[:, lanes] = unit
            gain = wide_ref[1:2, lanes]
            u2_ref[rows, lanes] = (unit * gain + wide_ref[2:3, lanes]).astype(BF16)
            du2 = lax.dot_general(
                cot_ref[rows, :], back_w_ref[lanes, :], NT, preferred_element_type=F32
            )
            broad_ref[0:1, lanes] += column_sum(du2 * unit)
            broad_ref[2:3, lanes] += column_sum(du2)
            grad = du2 * gain
            d_ref[:, lanes] = grad
            return (
                first + jnp.sum(grad, axis=1, keepdims=True),
                second + jnp.sum(grad * unit, axis=1, keepdims=True),
            )

        none = jnp.zeros((TILE, 1), F32)
        first, second = lax.fori_loop(0, FF // CHUNK, turn, (none, none))
        first = first / FF
        second = second / FF
        da_ref[...] = jnp.zeros_like(da_ref)

        def down(j, c):
            lanes = lanes_of(j)
            grad = scale * (d_ref[:, lanes] - first - g_ref[:, lanes] * second)
            df = (grad * slope_ref[:, lanes]).astype(BF16)
            df_ref[rows, lanes] = df
            broad_ref[1:2, lanes] += column_sum(df.astype(F32))
            da_ref[...] += lax.dot_general(
                df, in_w_ref[:, lanes], NT, preferred_element_type=F32
            )
            return c

        lax.fori_loop(0, FF // CHUNK, down, None)
        da2 = da_ref[...]
        unit_two, scale_two = norm_parts(x1_ref[...])
        narrow_ref[2:3, :] += column_sum(da2 * unit_two)
        narrow_ref[3:4, :] += column_sum(da2)
        cot = cot_ref[rows, :].astype(F32)
        dx = cot + norm_back(da2 * row_ref[3:4, :], unit_two, scale_two)
        dx_ref[rows, :] = dx
        datt = dx.astype(BF16)
        datt_ref[rows, :] = datt
        narrow_ref[4:5, :] += column_sum(datt.astype(F32))
        narrow_ref[5:6, :] += column_sum(cot)
        du = lax.dot_general(datt, out_w_ref[...], NT, preferred_element_type=F32)
        unit_one, scale_one = norm_parts(ctx_ref[rows, :].astype(F32))
        narrow_ref[0:1, :] += column_sum(du * unit_one)
        narrow_ref[1:2, :] += column_sum(du)
        do_ref[rows, :] = norm_back(du * row_ref[0:1, :], unit_one, scale_one).astype(BF16)
        mixed_ref[rows, :] = (
            jnp.dot(u2_ref[rows, :], back_w_ref[...], preferred_element_type=F32)
            + row_ref[5:6, :]
            + x1_ref[...]
        ).astype(BF16)
        return c

    lax.fori_loop(0, ctx_ref.shape[0] // TILE, tile, None)
    for m, ref in enumerate(do_refs):
        lanes = slice(m * HC, (m + 1) * HC)
        ref[...] = jnp.concatenate([do_ref[:half, lanes], do_ref[half:, lanes]], axis=1)


def middle(pieces, x, cot, narrow, wide, weights):
    n = x.shape[0]
    full = pl.BlockSpec(memory_space=VM)
    shape = jax.ShapeDtypeStruct
    scattered = len(weights) > 3
    weight_specs = [full] * len(weights)
    if scattered:
        weight_specs[0] = pl.BlockSpec(memory_space=SMEM)
    return pl.pallas_call(
        functools.partial(middle_kernel, scattered),
        name="middle",
        in_specs=[full] * (TP + 4) + weight_specs,
        out_specs=[full] * (TP + 9),
        out_shape=[shape(p.shape, BF16) for p in pieces]
        + [
            shape((n, D), BF16),
            shape((n, D), BF16),
            shape((n, D), BF16),
            shape((n, FF), BF16),
            shape((n, FF), BF16),
            shape((n, D), BF16),
            shape((n, D), F32),
            shape((8, D), F32),
            shape((8, FF), F32),
        ],
        scratch_shapes=[
            pltpu.VMEM((n, D), BF16),
            pltpu.VMEM((n, D), BF16),
            pltpu.VMEM((TILE, FF), F32),
            pltpu.VMEM((TILE, FF), F32),
            pltpu.VMEM((TILE, FF), F32),
            pltpu.VMEM((TILE, D), F32),
            pltpu.VMEM((TILE, D), F32),
        ]
        + ([pltpu.VMEM(s, BF16) for s in ((D, D), (D, FF), (FF, D))] if scattered else []),
        cost_estimate=cost(36),
    )(*pieces, x, cot, narrow, wide, *weights)


def layer_norm(values, gain, shift):
    average = jnp.mean(values, axis=-1, keepdims=True)
    centred = values - average
    variance = jnp.mean(centred * centred, axis=-1, keepdims=True)
    return centred * lax.rsqrt(variance + 1e-05) * gain + shift


def outer_sum(left, right):
    return lax.dot_general(left, right, (((0,), (0,)), ((), ())), preferred_element_type=F32)


def times_transposed(left, matrix):
    return lax.dot_general(left, matrix, (((1,), (1,)), ((), ())), preferred_element_type=F32)


def tie(value, *before):
    return lax.optimization_barrier((value, before))[0]


def pick(array, index, axis=0):
    return lax.dynamic_index_in_dim(array, index, axis, keepdims=False)


def make_local(ctx_size, fsdp_size):
    nq = ctx_size // TP
    fast = ctx_size == 8 and fsdp_size == 4

    def over_heads(value, mask):
        return lax.ppermute(
            value, "ctx", [(i, ((i // nq) ^ mask) * nq + i % nq) for i in range(ctx_size)]
        )

    def over_rows(value, shift):
        return lax.ppermute(
            value,
            "ctx",
            [(i, (i // nq) * nq + (i % nq - shift) % nq) for i in range(ctx_size)],
        )

    def over_fsdp(value, mask):
        return lax.ppermute(value, "fsdp", [(i, i ^ mask) for i in range(fsdp_size)])

    def over_split(value, masks):
        return lax.ppermute(
            value,
            "ctx",
            [(i, ((i // nq) ^ masks[i % nq]) * nq + i % nq) for i in range(ctx_size)],
        )

    moves = (over_heads, over_rows, over_fsdp, over_split)

    def exchange_heads(own, halves):
        one = over_heads(own, 1)
        two = over_heads(own, 2)
        first, second = halves
        low = over_heads(first(one), 2)
        high = over_heads(second(two), 1)
        return one, two, low, high

    def local(
        tokens,
        cotangent,
        lengths,
        dealing,
        qkv_weight,
        out_weight,
        in_weight,
        back_weight,
        norm_gains,
        shifts,
        ffn_gain,
        ffn_shifts,
    ):
        ctx = lax.axis_index("ctx")
        fs = lax.axis_index("fsdp")
        hg = ctx // nq
        qs = ctx % nq
        rows = tokens.shape[1]
        shard = qkv_weight.shape[0]
        deal_row = dealing[0]
        group_count = deal_row.shape[0]
        per = rows // GROUP
        bounds = jnp.cumsum(lengths[0])
        members = [
            [((hg ^ m) * nq + (qs + s) % nq) * per + j for m in range(TP) for j in range(per)]
            for s in range(nq)
        ]
        stored = jnp.stack([g for part in members for g in part]).astype(jnp.int32)
        onehot = (stored[:, None] == jnp.arange(group_count, dtype=jnp.int32)[None, :]).astype(
            jnp.int32
        )
        dealt = jnp.sum(onehot * deal_row[None, :], axis=1)
        mine = tokens[0]
        half = rows // 2
        one, two, low, high = exchange_heads(mine, (lambda a: a[:half], lambda a: a[half:]))
        chunks = (mine, one, two, low, high)

        def own_columns(weight):
            def take(at, size):
                value = weight[:, at : at + size]
                for g in range(1, TP):
                    other = weight[:, at + g * HC : at + g * HC + size]
                    value = jnp.where(hg == g, other, value)
                return value

            out = []
            for h in range(HPG):
                out += [take(D + h * DH, DH), take(2 * D + h * DH, DH)]
            return jnp.concatenate(out + [take(0, HC)], axis=1)

        feature = norm_gains.shape[1]
        narrow_rows = jnp.concatenate([norm_gains, shifts], axis=0)
        broad_rows = jnp.concatenate([ffn_gain[None], ffn_shifts], axis=0).reshape(12, feature)
        small = jnp.concatenate(
            [
                jnp.pad(narrow_rows, ((0, 6), (0, HC - feature))),
                jnp.pad(broad_rows, ((0, 4), (0, 2 * HC - feature))),
            ],
            axis=1,
        )
        packed = jnp.concatenate([own_columns(qkv_weight), small], axis=0)
        span = packed.shape[0] // nq
        piece = pick(packed.reshape(nq, span, 3 * HC), qs)
        came = [over_fsdp(piece, m) for m in range(1, fsdp_size)]
        parts = jnp.stack([piece] + came)
        shared = [over_rows(parts, s) for s in range(1, nq)]
        parts = jnp.stack([parts] + shared)
        ordered = [
            jnp.concatenate([pick(pick(parts, (h - qs) % nq), f ^ fs) for h in range(nq)], axis=0)
            for f in range(fsdp_size)
        ]
        w_own = jnp.concatenate([p[:shard] for p in ordered], axis=0)
        tails = [p[shard:] for p in ordered]
        narrow_all = jnp.concatenate([p[:10, :feature] for p in tails], axis=1).astype(F32)
        broad_all = jnp.concatenate(
            [p[:12, HC : HC + feature].reshape(3, -1) for p in tails], axis=1
        ).astype(F32)
        gains = narrow_all[:3]
        shift_rows = narrow_all[3:]
        ffn_scale = broad_all[0]
        ffn_shift_rows = broad_all[1:]

        if fast:
            gathered = gather_weights(
                in_weight, back_weight, out_weight, shared, (low, high), hg, qs, moves
            )
        else:
            in_w = lax.all_gather(in_weight, "fsdp", axis=0, tiled=True)
            back_w = lax.all_gather(back_weight, "fsdp", axis=0, tiled=True)
            out_w = lax.all_gather(out_weight, "fsdp", axis=0, tiled=True)
            out_blocks = out_w.reshape(TP, HC, D)
            out_rel = jnp.concatenate([pick(out_blocks, hg ^ m) for m in range(TP)], axis=0)

        def own_heads(row):
            return pick(row.reshape(TP, HC), hg)

        value_bias = own_heads(shift_rows[2]).reshape(HPG, DH)
        bias = jnp.concatenate(
            [
                jnp.stack([jnp.zeros((HPG, DH), F32), value_bias], axis=1).reshape(-1),
                own_heads(shift_rows[1]),
            ]
        )[None]
        norm_rows = jnp.stack([gains[0], shift_rows[0]])
        projected = [
            project(c, w_own, norm_rows, bias) for c in ((mine, one, two), (low, high))
        ]
        normed = [p[0] for p in projected]
        queries = [p[1] for p in projected]
        pairs = [p[2] for p in projected]
        for s in range(1, nq):
            pairs = pairs + [over_rows(p[2], s) for p in projected]
        if fast:
            dealt = tie(dealt, gathered[0])

        *context_parts, context_t, log_total, q_turned, kv_rows, kv_turned = attend_forward(
            dealt, bounds, queries, pairs
        )
        if fast:
            gathered = gather_rest(*gathered, log_total, moves)

        got = [context_parts[0]] + [over_heads(context_parts[m], m) for m in range(1, TP)]

        def relative(row):
            blocks = row.reshape(TP, HC)
            return jnp.concatenate([pick(blocks, hg ^ m) for m in range(TP)])

        narrow = jnp.stack(
            [relative(gains[1]), relative(shift_rows[3]), shift_rows[4], gains[2], shift_rows[5]]
            + [shift_rows[6]] * 3
        )
        wide = jnp.pad(
            jnp.stack([ffn_shift_rows[0], ffn_scale, ffn_shift_rows[1]]), ((0, 5), (0, 0))
        )
        cot = cotangent[0]
        if fast:
            weights = (weight_places(hg, qs, fs), in_weight, out_weight, back_weight, *gathered)
            w_axis = gather_columns(w_own, got, moves)
        else:
            weights = (in_w, out_rel, back_w)
        (
            *sent,
            mixed_out,
            inner_low,
            normed_two_low,
            inner_two_low,
            hidden_low,
            branch_low,
            grad_middle,
            narrow_sums,
            broad_sums,
        ) = middle(got, mine, cot, narrow, wide, weights)
        grad_gain_one, grad_shift_three, grad_gain_two, grad_shift_five = narrow_sums[:4]
        grad_out_bias, grad_back_bias = narrow_sums[4:6]
        grad_ffn_gain, grad_in_bias, grad_ffn_shift = broad_sums[:3]

        grad_rows = [sent[0]] + [over_heads(sent[m], m) for m in range(1, TP)]
        set_rows = TP * rows
        place = jnp.stack([hg, qs, fs]).astype(jnp.int32)
        if fast:
            keep, send = weight_grads(
                tie(place, w_axis), inner_low, branch_low, normed_two_low, hidden_low, inner_two_low, cot
            )
            stage = first_stage(keep, send, moves)

        def backward_of(h, table):
            return attend_backward(
                h, table, bounds, q_turned, kv_rows, kv_turned, context_t, log_total, grad_rows
            )

        def exchange(other):
            return [
                over_rows(other[(s - 1) * set_rows : s * set_rows], nq - s) for s in range(1, nq)
            ]

        table = tie(dealt, keep) if fast else dealt
        results = [backward_of(0, table)]
        cames = [exchange(results[0][2])]
        for h in range(1, HPG):
            table = dealt
            if fast and h == 1:
                table = tie(dealt, results[0], stage)
                corners = gather_corners(tie(w_axis, results[0]), qs, moves)
            elif fast:
                w_parts = select_columns(w_axis, corners, qs, moves)
                table = tie(dealt, results[h - 1], w_parts)
            results.append(backward_of(h, table))
            cames.append(exchange(results[h][2]))
        if fast:
            second = second_stage(stage, results[-1], moves)
            cames = tie(cames, second)
        came = [cames[h][s] for s in range(nq - 1) for h in range(HPG)]
        *grads, sums = finish([r[0] for r in results], [r[1] for r in results], came)

        back_parts = [grads[0]] + [over_heads(grads[m], m) for m in range(1, TP)]
        if not fast:
            w_one, w_two, w_low, w_high = exchange_heads(
                w_own, (lambda a: a[: D // 2], lambda a: a[D // 2 :])
            )
            w_parts = (w_one, w_two, jnp.concatenate([w_low, w_high], axis=0))
        grad_normed = sum(
            times_transposed(g, w) for g, w in zip(back_parts, (w_own,) + tuple(w_parts))
        )
        inputs = mine.astype(F32)
        first_pull = jax.vjp(layer_norm, inputs, gains[0], shift_rows[0])[1]
        grad_inputs_part, grad_gain_zero, grad_shift_zero = first_pull(grad_normed)
        input_grad = grad_middle + grad_inputs_part

        def absolute(row):
            blocks = row.reshape(TP, HC)
            return jnp.concatenate([pick(blocks, hg ^ m) for m in range(TP)])

        order = ctx * fsdp_size + fs
        total_devices = ctx_size * fsdp_size
        if fast:
            zero = jnp.zeros((D,), F32)
            narrow = [
                zero,
                zero,
                absolute(grad_gain_one),
                grad_gain_two,
                zero,
                zero,
                absolute(grad_shift_three),
                grad_out_bias,
                grad_shift_five,
                grad_back_bias,
            ]
            broad = [
                v.reshape(total_devices, 4, D // total_devices).transpose(1, 0, 2).reshape(4, D)
                for v in (grad_ffn_gain, grad_in_bias, grad_ffn_shift)
            ]
            extra = jnp.concatenate(
                [jnp.stack(narrow)] + broad + [jnp.zeros((42, D), F32)], axis=0
            ).T
            norm_columns = jnp.pad(norm_rows, ((0, 6), (0, 0))).T
            kept, sent_columns = columns(
                place, normed, grads, w_own, sums, norm_columns, extra
            )
            qkv_out, tail = reduce_columns(kept, sent_columns, hg, fs, moves)
            turned = tail.T
            small_out = (
                jnp.stack([turned[0], turned[2], turned[3]]),
                jnp.concatenate([turned[1:2], turned[4:10]], axis=0),
                turned[10:14].reshape(-1),
                turned[14:22].reshape(2, -1),
            )
            back_out, in_out, out_out = later_stages(second, fs, moves)
        else:

            def placed(row):
                blank = jnp.zeros((TP, HC), F32)
                return lax.dynamic_update_slice(blank, row[None], (hg, 0)).reshape(-1)

            row = sums[0]
            value_sums = row[:WIDE].reshape(HPG, 2, DH)[:, 1].reshape(-1)
            small_terms = jnp.concatenate(
                [
                    grad_gain_zero,
                    absolute(grad_gain_one),
                    grad_gain_two,
                    grad_shift_zero,
                    placed(row[WIDE:]),
                    placed(value_sums),
                    absolute(grad_shift_three),
                    grad_out_bias,
                    grad_shift_five,
                    grad_back_bias,
                    grad_ffn_gain,
                    grad_in_bias,
                    grad_ffn_shift,
                ]
            )
            axes = ("ctx", "fsdp")
            small_terms = lax.psum(small_terms, axes)
            narrow = small_terms[: 10 * D].reshape(10, total_devices, D // total_devices)
            narrow = pick(narrow, order, 1)
            broad = small_terms[10 * D :].reshape(3, total_devices, FF // total_devices)
            broad = pick(broad, order, 1)
            small_out = (narrow[:3], narrow[3:], broad[0], broad[1:])
            blocks = outer_sum(inner_low, branch_low).reshape(TP, HC, D)
            grad_out_w = jnp.concatenate([pick(blocks, hg ^ m) for m in range(TP)], axis=0)
            grad_in_w = outer_sum(normed_two_low, hidden_low)
            grad_back_w = outer_sum(inner_two_low, cot)
            back_out, in_out, out_out = (
                lax.psum_scatter(g.astype(BF16), axes, scatter_dimension=0, tiled=True).astype(F32)
                for g in (grad_back_w, grad_in_w, grad_out_w)
            )
            grad_qkv_w = outer_sum(jnp.concatenate(normed, axis=0), jnp.concatenate(grads, axis=0))
            pairs_w = grad_qkv_w[:, :WIDE].reshape(D, HPG, 2, DH)
            three = jnp.stack(
                [
                    grad_qkv_w[:, WIDE:],
                    pairs_w[:, :, 0].reshape(D, HC),
                    pairs_w[:, :, 1].reshape(D, HC),
                ],
                axis=1,
            )
            blank = jnp.zeros((D, 3, TP, HC), BF16)
            whole = lax.dynamic_update_slice(
                blank, three.astype(BF16)[:, :, None], (0, 0, hg, 0)
            ).reshape(D, 3 * D)
            qkv_out = lax.psum_scatter(whole, axes, scatter_dimension=0, tiled=True).astype(F32)
        return (
            mixed_out[None],
            input_grad[None],
            qkv_out,
            out_out,
            in_out,
            back_out,
        ) + small_out

    return local


def gather_weights(in_weight, back_weight, out_weight, first, then, hg, qs, moves):
    over_heads, over_rows, over_fsdp, over_split = moves
    c = hg * 2 + qs
    cut = lax.dynamic_slice(in_weight, (0, c * 384), (192, 384))
    out_cut = lax.dynamic_slice(out_weight, (hg * 48, qs * 384), (48, 384))
    piece = jnp.concatenate(
        [
            jnp.concatenate([cut[:96], cut[96:]], axis=1),
            pick(back_weight.reshape(8, 96, D), c),
            jnp.concatenate([out_cut[:24], out_cut[24:]], axis=1),
        ],
        axis=0,
    )
    piece = tie(piece, *first)
    foreign = jnp.stack([over_fsdp(piece, m) for m in (1, 2, 3)])
    near = jnp.stack([foreign, over_rows(foreign, 1)])
    return near, over_split(tie(near, *then), (1, 2))


def gather_rest(near, axis, before, moves):
    over_heads, over_rows, over_fsdp, over_split = moves
    axis = tie(axis, before)
    corner = over_split(axis[0], (2, 1))
    return near, axis, over_rows(axis, 1), corner, over_rows(corner, 1)


def weight_places(hg, qs, fs):
    near_x = jnp.where(qs == 0, 1, 2)
    far_x = 3 - near_x
    return jnp.stack(
        [fs ^ m for m in range(4)]
        + [fs ^ m ^ hg for m in range(4)]
        + [hg * 2 + qs, hg * 2 + 1 - qs]
        + [(hg ^ near_x) * 2 + qs, (hg ^ near_x) * 2 + 1 - qs]
        + [(hg ^ far_x) * 2 + 1 - qs, (hg ^ far_x) * 2 + qs]
        + [(hg ^ 3) * 2 + qs, (hg ^ 3) * 2 + 1 - qs]
    ).astype(jnp.int32)


def gather_columns(weight, before, moves):
    over_heads, over_rows, over_fsdp, over_split = moves
    return over_split(tie(weight, before), (1, 2))


def gather_corners(axis, qs, moves):
    over_heads, over_rows, over_fsdp, over_split = moves
    return over_split(pick(axis.reshape(2, D // 2, -1), qs), (2, 1))


def select_columns(axis, corner, qs, moves):
    over_heads, over_rows, over_fsdp, over_split = moves
    axis_far = over_rows(axis, 1)
    corner_far = over_rows(corner, 1)
    even = qs == 0
    one = jnp.where(even, axis, axis_far)
    two = jnp.where(even, axis_far, axis)
    three = jnp.concatenate(
        [jnp.where(even, corner, corner_far), jnp.where(even, corner_far, corner)], axis=0
    )
    return one, two, three


CUT = 432


def first_stage(keep, send, moves):
    over_heads, over_rows, over_fsdp, over_split = moves
    came = over_rows(send, 1)

    def added(block, rows):
        return (keep[block, rows].astype(F32) + came[block, rows].astype(F32)).astype(BF16)

    top = slice(0, CUT)
    bottom = slice(CUT, 2 * CUT)
    first_send = jnp.stack([added(1, top), added(3, top)])
    first_keep = jnp.stack([added(0, top), added(2, top)])
    second_send = jnp.stack([added(2, bottom), added(3, bottom)])
    second_keep = jnp.stack([added(0, bottom), added(1, bottom)])
    return first_send, first_keep, second_send, second_keep


def added(mine, came):
    return (mine.astype(F32) + came.astype(F32)).astype(BF16)


def second_stage(stage, before, moves):
    over_heads, over_rows, over_fsdp, over_split = moves
    first_send, first_keep, second_send, second_keep = stage
    first_keep, second_keep = tie((first_keep, second_keep), before)
    first_came = over_heads(first_send, 1)
    second_came = over_heads(second_send, 2)
    return (
        added(first_keep[0], first_came[0]),
        added(first_keep[1], first_came[1]),
        added(second_keep[0], second_came[0]),
        added(second_keep[1], second_came[1]),
    )


def later_stages(stage, fs, moves):
    over_heads, over_rows, over_fsdp, over_split = moves
    first, first_send, second, second_send = stage
    first_last = over_heads(first_send, 2)
    second_last = over_heads(second_send, 1)
    whole = jnp.concatenate([added(first, first_last), added(second, second_last)], axis=0)
    back = whole[:384].reshape(4, 96, D)
    inner = whole[384:768].reshape(4, 4, 24, D)
    out = whole[768:].reshape(4, 24, D)

    def piece(f):
        return jnp.concatenate(
            [pick(back, f), pick(inner, f, 1).reshape(96, D), pick(out, f)], axis=0
        )

    total = piece(fs).astype(F32)
    for m in (1, 2, 3):
        total = total + over_fsdp(piece(fs ^ m), m).astype(F32)
    inner = jnp.concatenate([total[96 + 24 * j : 120 + 24 * j] for j in range(4)], axis=1)
    return total[:96], inner, total[192:216]


def reduce_columns(keep, send, hg, fs, moves):
    over_heads, over_rows, over_fsdp, over_split = moves
    kept = keep + over_rows(send, 1)
    kept = kept.reshape(TP, 4, 24, 640)
    low = kept.astype(BF16)
    total = pick(kept, fs, 1)
    for m in (1, 2, 3):
        total = total + over_fsdp(pick(low, fs ^ m, 1), m).astype(F32)
    mine = jnp.stack(
        [pick(total, hg)] + [over_heads(pick(total, hg ^ m), m) for m in (1, 2, 3)]
    )
    tail = jnp.sum(mine[:, :, 3 * HC :], axis=0)
    mine = [pick(mine, hg ^ g) for g in range(TP)]
    out = [block[:, WIDE : 3 * HC] for block in mine]
    for part in range(2):
        for block in mine:
            for h in range(HPG):
                at = h * HW + part * DH
                out.append(block[:, at : at + DH])
    return jnp.concatenate(out, axis=1), tail


def solution(mesh):
    ctx_size = mesh.shape["ctx"]
    fsdp_size = mesh.shape["fsdp"]
    in_specs = (
        P("fsdp", "ctx", None),
        P("fsdp", "ctx", None),
        P("fsdp", None),
        P("fsdp", None),
        P("fsdp", None),
        P("fsdp", None),
        P("fsdp", None),
        P("fsdp", None),
        P(None, "fsdp"),
        P(None, "fsdp"),
        P("fsdp"),
        P(None, "fsdp"),
    )
    out_specs = (
        P("fsdp", "ctx", None),
        P("fsdp", "ctx", None),
        P(("ctx", "fsdp"), None),
        P(("ctx", "fsdp"), None),
        P(("ctx", "fsdp"), None),
        P(("ctx", "fsdp"), None),
        P(None, ("ctx", "fsdp")),
        P(None, ("ctx", "fsdp")),
        P(("ctx", "fsdp")),
        P(None, ("ctx", "fsdp")),
    )
    return jax.shard_map(
        make_local(ctx_size, fsdp_size),
        mesh=mesh,
        in_specs=in_specs,
        out_specs=out_specs,
        check_vma=False,
    )
```

time: 1470 us -> 410 us (0.28)
  waiting for transfers between devices: 720 us -> 77.5 us
  matrix products: 403 us -> 5.99 us
  Pallas kernels: 0 us -> 184 us
  blocking collectives: 94.2 us -> 0 us
  local copies, waits for them, and re-layouts: 131 us -> 43 us
  other arithmetic: 95.9 us -> 43.5 us
  starting transfers between devices: 0.91 us -> 48.3 us
    reduce_scatter x6 -> x0, waiting for transfers between devices: 550 us -> none  [the longest x1 142 us: local(): lax.psum_scatter(grad_in_w, ('ctx', 'fsdp'), scatter_dimension=0, tiled=T...]
    dot_general x64 -> x0, matrix products: 383 us -> none  [the longest x8 67.5 us: grad_pair(): jnp.einsum('qhd,khd->hqk', grad_rows, value3, preferred_element_type=jnp....]
    pallas_call x0 -> x10, Pallas kernels: none -> 184 us  [the longest x3 65.9 us: attend_backward(): pl.pallas_call(functools.partial(backward_kernel, h), name='attend_backwa...]
    unnamed x14 -> x0, waiting for transfers between devices: 89.9 us -> none
    reduce_sum x21 -> x2, other arithmetic: 81.8 us -> 0.77 us  [the longest x1 0.69 us: local(): dealt = jnp.sum(onehot * deal_row[None, :], axis=1)]
    all_gather x6 -> x0, waiting for transfers between devices: 80.4 us -> none  [the longest x1 43.6 us: local(): lax.all_gather(qkv_weight, 'fsdp', axis=0, tiled=True)]
    ppermute x0 -> x49, waiting for transfers between devices: none -> 77.5 us  [the longest x12 30.9 us: over_fsdp(): lax.ppermute(value, 'fsdp', [(i, i ^ mask) for i in range(fsdp_size)])]
    all_gather x4 -> x0, blocking collectives: 53.5 us -> none  [the longest x1 14.9 us: local(): lax.all_gather(shifts, 'fsdp', axis=1, tiled=True)]
  transfers between devices with their start and end apart: 13 -> 49, of which waited for: 10 -> 17; matrix products, arithmetic and copies ran while one was open for 21% -> 19% of each run, Pallas kernels for 0% -> 32%
where the time goes in v1:
time: 410 us; the launch traced here: 404 us
  Pallas kernels  184 us (45%)
  waiting for transfers between devices  77.5 us (19%)
  starting transfers between devices  48.3 us (12%)
  other arithmetic  43.5 us (11%)
  local copies, waits for them, and re-layouts  43 us (10%)
  matrix products  5.99 us (1%)
    pallas_call x3, Pallas kernels, attend_backward(): pl.pallas_call(functools.partial(backward_kernel, h), name='attend_backwa...  65.9 us
    pallas_call x1, Pallas kernels, attend_forward(): pl.pallas_call(functools.partial(forward_kernel, len(queries), len(pairs)...  42.9 us
    pallas_call x1, Pallas kernels, middle(): pl.pallas_call(functools.partial(middle_kernel, scattered), name='middle'...  35 us
    ppermute x12, waiting for transfers between devices, over_fsdp(): lax.ppermute(value, 'fsdp', [(i, i ^ mask) for i in range(fsdp_size)])  30.9 us
    ppermute x4, waiting for transfers between devices, over_split(): lax.ppermute(value, 'ctx', [(i, (i // nq ^ masks[i % nq]) * nq + i % nq)...  26.5 us
    ppermute x20, starting transfers between devices, over_heads(): lax.ppermute(value, 'ctx', [(i, (i // nq ^ mask) * nq + i % nq) for i in...  24.3 us
    ppermute x12, starting transfers between devices, over_fsdp(): lax.ppermute(value, 'fsdp', [(i, i ^ mask) for i in range(fsdp_size)])  19.1 us
    pallas_call x1, Pallas kernels, weight_grads(): pl.pallas_call(weight_grads_kernel, name='weight_grads', in_specs=[pl.Blo...  14.6 us
  transfers between devices with their start and end apart: 49, of which 17 were waited for; matrix products, arithmetic and copies ran while one was open for 19% of the time, Pallas kernels for 32%

profile of v1, /device:TPU:0, one launch (start us, length us, event | category | flops | bytes accessed | tf_op | source)
XLA Modules:
  0.0 404.0 jit_solution(2913684892198166250)
XLA Ops:
  4.8 5.1 %collective-permute-start.2 = (bf16[104,576]{1,0:T(8,128)(2,1)S(1)}, bf16[104,576]{1,0:T(8,128)(2,1)S(1)}, u32[]{:S(2)}, u32[]{:S(2)}) collective-permute-start(bf16[104,576]{1,0:T(8,128)(2,1)S(1)} %fusion.72), channel_id=1, source_target_pairs={{0,3},{1,2},{2,1},{3,0},{4,7},{5,6},{6,5},{7,4},{8,11},{9,10},{10,... | collective-permute-start | bytes 359432 | tf_op jit(solution)/shard_map/ppermute | solution.py:804
  10.6 3.8 collective-permute-done.2
  14.4 6.8 %collective-permute-done.1 = bf16[104,576]{1,0:T(8,128)(2,1)S(1)} collective-permute-done((bf16[104,576]{1,0:T(8,128)(2,1)S(1)}, bf16[104,576]{1,0:T(8,128)(2,1)S(1)}, u32[]{:S(2)}, u32[]{:S(2)}) %collective-permute-start.1) | collective-permute-done | bytes 119840 | tf_op jit(solution)/shard_map/ppermute | solution.py:804
  35.2 5.6 %fusion.12.refs_3_.refs_2_.refs_6_ = bf16[768,576]{1,0:T(8,128)(2,1)} fusion(bf16[104,576]{1,0:T(8,128)(2,1)S(1)} %bitcast.210, bf16[104,576]{1,0:T(8,128)(2,1)S(1)} %get-tuple-element.198, bf16[104,576]{1,0:T(8,128)(2,1)S(1)} %bitcast.209, bf16[104,576]{1,0:T(8,128)(2,1)S(1)} %get-tuple-element.197, bf16[104,576]{1,0:T(8,128)(2,1)S(1)} %bitcast.208, ...), kind=kLoop, calls=%fused_computation.59 | loop fusion | flops 11501568 | bytes 1843200 | tf_op jit(solution)/shard_map/concatenate | solution.py:895
  47.3 8.0 %project.2 = (bf16[1536,768]{1,0:T(8,128)(2,1)}, bf16[1536,384]{1,0:T(8,128)(2,1)}, bf16[1536,384]{1,0:T(8,128)(2,1)}) custom-call(bf16[512,768]{1,0:T(8,128)(2,1)} %bitcast.192, bf16[512,768]{1,0:T(8,128)(2,1)} %collective-permute-done.8.refs_1_, bf16[512,768]{1,0:T(8,128)(2,1)} %collective-permute-done.9.refs_2_, ...), custom_call_target="tpu_custom_call" | custom-call | flops 7699999744 | bytes 100000 | tf_op jit(solution)/shard_map/project/pallas_call | solution.py:101
  68.2 42.9 %attend_forward.1 = (bf16[256,384]{1,0:T(8,128)(2,1)}, bf16[256,384]{1,0:T(8,128)(2,1)}, bf16[256,384]{1,0:T(8,128)(2,1)}, bf16[256,384]{1,0:T(8,128)(2,1)}, f32...) custom-call(s32[16]{0:T(128)} %select_reduce_fusion.refs_0_.dealt_re, ...), custom_call_target="tpu_custom_call" | custom-call | flops 39600001024 | bytes 100000 | tf_op jit(solution)/shard_map/attend_forward/pallas_call | solution.py:194
  118.6 14.7 %collective-permute-done.19.refs_15_ = bf16[3,216,768]{2,1,0:T(8,128)(2,1)} collective-permute-done((bf16[3,216,768]{2,1,0:T(8,128)(2,1)S(1)}, bf16[3,216,768]{2,1,0:T(8,128)(2,1)}, u32[]{:S(2)}, u32[]{:S(2)}) %collective-permute-start.19) | collective-permute-done | bytes 995360 | tf_op jit(solution)/shard_map/ppermute | solution.py:807
  140.6 9.8 %collective-permute-done.21 = bf16[768,576]{0,1:T(8,128)(2,1)S(1)} collective-permute-done((bf16[768,576]{0,1:T(8,128)(2,1)S(1)}, bf16[768,576]{0,1:T(8,128)(2,1)S(1)}, u32[]{:S(2)}, u32[]{:S(2)}) %collective-permute-start.21) | collective-permute-done | bytes 884768 | tf_op jit(solution)/shard_map/ppermute | solution.py:807
  150.4 35.0 %middle.1 = (bf16[256,384]{1,0:T(8,128)(2,1)}, bf16[256,384]{1,0:T(8,128)(2,1)}, bf16[256,384]{1,0:T(8,128)(2,1)}, bf16[256,384]{1,0:T(8,128)(2,1)}, bf16[512,76...) custom-call(bf16[256,384]{1,0:T(8,128)(2,1)} %get-tuple-element.77.r, ...), custom_call_target="tpu_custom_call" | custom-call | flops 39600001024 | bytes 100000 | tf_op jit(solution)/shard_map/middle/pallas_call | solution.py:733
  185.4 14.6 %weight_grads.1 = (bf16[4,864,768]{2,1,0:T(8,128)(2,1)}, bf16[4,864,768]{2,1,0:T(8,128)(2,1)}) custom-call(s32[3]{0:T(128)} %pad_add_fusion.place_ref, bf16[512,768]{1,0:T(8,128)(2,1)} %get-tuple-element.88.u_ref, bf16[512,768]{1,0:T(8,128)(2,1)} %get-tuple-element.89.datt_ref, bf16[512,768]{1,0:T(8,128)(2,1)} %get-tuple-element.90.a2_ref, ...), custom_call_target="tpu_custom_call" | custom-call | flops 15399999488 | bytes 100000 | tf_op jit(solution)/shard_map/weight_grads/pallas_call | solution.py:512
  201.7 6.7 %collective-permute-done.26 = bf16[768,576]{0,1:T(8,128)(2,1)S(1)} collective-permute-done((bf16[768,576]{0,1:T(8,128)(2,1)S(1)}, bf16[768,576]{0,1:T(8,128)(2,1)S(1)}, u32[]{:S(2)}, u32[]{:S(2)}) %collective-permute-start.26) | collective-permute-done | bytes 884768 | tf_op jit(solution)/shard_map/ppermute | solution.py:797
  213.3 4.3 %collective-permute-done.22.refs_1_ = bf16[256,384]{1,0:T(8,128)(2,1)S(1)} collective-permute-done((bf16[256,384]{1,0:T(8,128)(2,1)}, bf16[256,384]{1,0:T(8,128)(2,1)S(1)}, u32[]{:S(2)}, u32[]{:S(2)}) %collective-permute-start.22) | collective-permute-done | bytes 196640 | tf_op jit(solution)/shard_map/ppermute | solution.py:792
  217.7 4.5 %collective-permute-done.23.refs_2_ = bf16[256,384]{1,0:T(8,128)(2,1)S(1)} collective-permute-done((bf16[256,384]{1,0:T(8,128)(2,1)S(1)}, bf16[256,384]{1,0:T(8,128)(2,1)S(1)}, u32[]{:S(2)}, u32[]{:S(2)}) %collective-permute-start.23) | collective-permute-done | bytes 196640 | tf_op jit(solution)/shard_map/ppermute | solution.py:792
  222.9 21.9 %attend_backward.3 = (bf16[2048,64]{1,0:T(8,128)(2,1)}, f32[2048,128]{1,0:T(8,128)}, bf16[2048,128]{1,0:T(8,128)(2,1)}) custom-call(s32[16]{0:T(128)} %select_reduce_fusion.refs_0_.dealt_ref, s32[4]{0:T(128)} %bitcast.257, bf16[384,2048]{1,0:T(8,128)(2,1)} %get-tuple-element.95.qt_ref, bf16[4096,384]{1,0:T(8,128)(2,1)} %get-tuple-element.96.kv_ref, ...), custom_call_target="tpu_custom_call" | custom-call | flops 20899999744 | bytes 100000 | tf_op jit(solution)/shard_map/attend_backward/pallas_call | solution.py:287
  254.5 5.1 %add_convert_fusion.7 = (bf16[1,432,768]{2,1,0:T(8,128)(2,1)S(1)}, bf16[1,432,768]{2,1,0:T(8,128)(2,1)S(1)}, bf16[1,432,768]{2,1,0:T(8,128)(2,1)S(1)}, bf16[1,43...) fusion(bf16[4,864,768]{2,1,0:T(8,128)(2,1)} %collective-permute, ...), kind=kLoop, calls=%fused_computation.48 | loop fusion | flops 10616832 | bytes 15925248 | tf_op jit(solution)/shard_map/convert_element_type | solution.py:1209
  264.1 22.2 %attend_backward.4 = (bf16[2048,64]{1,0:T(8,128)(2,1)}, f32[2048,128]{1,0:T(8,128)}, bf16[2048,128]{1,0:T(8,128)(2,1)}) custom-call(s32[16]{0:T(128)} %select_reduce_fusion.refs_0_.dealt_ref, s32[4]{0:T(128)} %bitcast.258, bf16[384,2048]{1,0:T(8,128)(2,1)} %get-tuple-element.95.qt_ref, bf16[4096,384]{1,0:T(8,128)(2,1)} %get-tuple-element.96.kv_ref, ...), custom_call_target="tpu_custom_call" | custom-call | flops 20899999744 | bytes 100000 | tf_op jit(solution)/shard_map/attend_backward/pallas_call | solution.py:287
  286.3 21.8 %attend_backward.5 = (bf16[2048,64]{1,0:T(8,128)(2,1)}, f32[2048,128]{1,0:T(8,128)}, bf16[2048,128]{1,0:T(8,128)(2,1)}) custom-call(s32[16]{0:T(128)} %select_reduce_fusion.refs_0_.dealt_ref, s32[4]{0:T(128)} %bitcast.259, bf16[384,2048]{1,0:T(8,128)(2,1)} %get-tuple-element.95.qt_ref, bf16[4096,384]{1,0:T(8,128)(2,1)} %get-tuple-element.96.kv_ref, ...), custom_call_target="tpu_custom_call" | custom-call | flops 20899999744 | bytes 100000 | tf_op jit(solution)/shard_map/attend_backward/pallas_call | solution.py:287
  319.9 4.1 %concatenate.111 = f32[64,768]{0,1:T(8,128)} concatenate(f32[2,768]{0,1:T(8,128)S(1)} %broadcast.60, f32[1,768]{0,1:T(8,128)S(1)} %copy-done.11, f32[1,768]{0,1:T(8,128)S(1)} %copy-done.12, f32[2,768]{0,1:T(8,128)S(1)} %broadcast.60, f32[1,768]{0,1:T(8,128)} %stack.285, f32[1,768]{0,1:T(8,128)} %copy.149, f32[1,768]{0,1:T(8,128)} %copy.150, f32[1,768]{0,1:T(8,128)} %copy.151, ...), dimensions={0} | concatenate | bytes 393216 | tf_op jit(solution)/shard_map/concatenate | solution.py:1056
  330.1 5.8 %finish.1 = (bf16[512,576]{1,0:T(8,128)(2,1)}, bf16[512,576]{1,0:T(8,128)(2,1)}, bf16[512,576]{1,0:T(8,128)(2,1)}, bf16[512,576]{1,0:T(8,128)(2,1)}, f32[8,576]{1,0:T(8,128)}) custom-call(bf16[2048,64]{1,0:T(8,128)(2,1)} %get-tuple-element.103.refs_0_, bf16[2048,64]{1,0:T(8,128)(2,1)} %get-tuple-element.108.refs_1_, ...), custom_call_target="tpu_custom_call" | custom-call | flops 6600000000 | bytes 100000 | tf_op jit(solution)/shard_map/finish/pallas_call | solution.py:349
  344.7 4.4 %collective-permute-start.46 = (bf16[216,768]{1,0:T(8,128)(2,1)}, bf16[216,768]{1,0:T(8,128)(2,1)}, u32[]{:S(2)}, u32[]{:S(2)}) collective-permute-start(bf16[216,768]{1,0:T(8,128)(2,1)} %pad_maximum_fusion.10), channel_id=1, source_target_pairs={{0,1},{1,0},{2,3},{3,2},{4,5},{5,4},{6,7},{7,6},{8,9},{9,8},{10,11... | collective-permute-start | bytes 995336 | tf_op jit(solution)/shard_map/ppermute | solution.py:804
  349.0 8.4 %columns.1 = (f32[4,96,640]{2,1,0:T(8,128)}, f32[4,96,640]{2,1,0:T(8,128)}) custom-call(s32[3]{0:T(128)} %pad_add_fusion.place_ref, bf16[1536,768]{1,0:T(8,128)(2,1)} %get-tuple-element.125.refs_0_, bf16[512,768]{1,0:T(8,128)(2,1)} %get-tuple-element.126.refs_1_, bf16[512,576]{1,0:T(8,128)(2,1)} %get-tuple-element.121.refs_2_, ...), custom_call_target="tpu_custom_call" | custom-call | flops 8800000000 | bytes 100000 | tf_op jit(solution)/shard_map/columns/pallas_call | solution.py:410
  359.8 8.9 %collective-permute-done.47 = bf16[216,768]{1,0:T(8,128)(2,1)} collective-permute-done((bf16[216,768]{1,0:T(8,128)(2,1)S(1)}, bf16[216,768]{1,0:T(8,128)(2,1)}, u32[]{:S(2)}, u32[]{:S(2)}) %collective-permute-start.47) | collective-permute-done | bytes 331808 | tf_op jit(solution)/shard_map/ppermute | solution.py:804
  383.7 3.7 collective-permute-done.40
  387.3 4.7 %collective-permute-done.39 = bf16[4,24,640]{2,1,0:T(8,128)(2,1)S(1)} collective-permute-done((bf16[4,24,640]{2,1,0:T(8,128)(2,1)S(1)}, bf16[4,24,640]{2,1,0:T(8,128)(2,1)S(1)}, u32[]{:S(2)}, u32[]{:S(2)}) %collective-permute-start.39) | collective-permute-done | bytes 122912 | tf_op jit(solution)/shard_map/ppermute | solution.py:804
  (329 shorter events, 129.6 us)
Async XLA Ops:
  21.4 20.1 %collective-permute-start.8 = (bf16[512,768]{1,0:T(8,128)(2,1)S(1)}, bf16[512,768]{1,0:T(8,128)(2,1)}, u32[]{:S(2)}, u32[]{:S(2)}) collective-permute-start(bf16[512,768]{1,0:T(8,128)(2,1)S(1)} %bitcast.194), channel_id=1, source_target_pairs={{0,8},{4,12},{8,0},{12,4},{16,24},{20,28},{24,16},{28,20},{1,9},{5... | collective-permute-start | bytes 2359304 | tf_op jit(solution)/shard_map/ppermute | solution.py:792
  23.0 21.1 %collective-permute-start.9 = (bf16[512,768]{1,0:T(8,128)(2,1)S(1)}, bf16[512,768]{1,0:T(8,128)(2,1)}, u32[]{:S(2)}, u32[]{:S(2)}) collective-permute-start(bf16[512,768]{1,0:T(8,128)(2,1)S(1)} %bitcast.195), channel_id=1, source_target_pairs={{0,16},{4,20},{8,24},{12,28},{16,0},{20,4},{24,8},{28,12},{1,17},{... | collective-permute-start | bytes 2359304 | tf_op jit(solution)/shard_map/ppermute | solution.py:792
  27.8 27.5 %collective-permute-start.6 = (bf16[216,768]{1,0:T(8,128)(2,1)}, bf16[216,768]{1,0:T(8,128)(2,1)}, u32[]{:S(2)}, u32[]{:S(2)}) collective-permute-start(bf16[216,768]{1,0:T(8,128)(2,1)} %maximum_maximum_fusion), channel_id=1, source_target_pairs={{0,3},{1,2},{2,1},{3,0},{4,7},{5,6},{6,5},{7,4},{8,11},{9,10},{10,... | collective-permute-start | bytes 995336 | tf_op jit(solution)/shard_map/ppermute | solution.py:804
  30.3 28.0 %collective-permute-start.5 = (bf16[216,768]{1,0:T(8,128)(2,1)}, bf16[216,768]{1,0:T(8,128)(2,1)}, u32[]{:S(2)}, u32[]{:S(2)}) collective-permute-start(bf16[216,768]{1,0:T(8,128)(2,1)} %maximum_maximum_fusion), channel_id=1, source_target_pairs={{0,2},{1,3},{2,0},{3,1},{4,6},{5,7},{6,4},{7,5},{8,10},{9,11},{10,... | collective-permute-start | bytes 995336 | tf_op jit(solution)/shard_map/ppermute | solution.py:804
  30.3 28.0 %collective-permute-start.4 = (bf16[216,768]{1,0:T(8,128)(2,1)}, bf16[216,768]{1,0:T(8,128)(2,1)}, u32[]{:S(2)}, u32[]{:S(2)}) collective-permute-start(bf16[216,768]{1,0:T(8,128)(2,1)} %maximum_maximum_fusion), channel_id=1, source_target_pairs={{0,1},{1,0},{2,3},{3,2},{4,5},{5,4},{6,7},{7,6},{8,9},{9,8},{10,11... | collective-permute-start | bytes 995336 | tf_op jit(solution)/shard_map/ppermute | solution.py:804
  42.5 17.3 %collective-permute-start.10 = (bf16[256,768]{1,0:T(8,128)(2,1)S(1)}, bf16[256,768]{1,0:T(8,128)(2,1)}, u32[]{:S(2)}, u32[]{:S(2)}) collective-permute-start(bf16[256,768]{1,0:T(8,128)(2,1)S(1)} %slice.583), channel_id=1, source_target_pairs={{0,16},{4,20},{8,24},{12,28},{16,0},{20,4},{24,8},{28,12},{1,17},{... | collective-permute-start | bytes 1179656 | tf_op jit(solution)/shard_map/ppermute | solution.py:792
  67.6 43.5 %collective-permute-start.17 = (bf16[2,3,216,768]{3,2,1,0:T(8,128)(2,1)S(1)}, bf16[2,3,216,768]{3,2,1,0:T(8,128)(2,1)}, u32[]{:S(2)}, u32[]{:S(2)}) collective-permute-start(bf16[2,3,216,768]{3,2,1,0:T(8,128)(2,1)S(1)} %pad_maximum_fusion.refs_12_), channel_id=1, source_target_pairs={{0,8},{4,20},{8,0},{12,28},{16,24},{20,4},{24,16},{28,12},{1,9},{5... | collective-permute-start | bytes 5971976 | tf_op jit(solution)/shard_map/ppermute | solution.py:807
  112.5 20.7 %collective-permute-start.19 = (bf16[3,216,768]{2,1,0:T(8,128)(2,1)S(1)}, bf16[3,216,768]{2,1,0:T(8,128)(2,1)}, u32[]{:S(2)}, u32[]{:S(2)}) collective-permute-start(bf16[3,216,768]{2,1,0:T(8,128)(2,1)S(1)} %slice_bitcast_fusion), channel_id=1, source_target_pairs={{0,16},{4,12},{8,24},{12,4},{16,0},{20,28},{24,8},{28,20},{1,17},{... | collective-permute-start | bytes 2985992 | tf_op jit(solution)/shard_map/ppermute | solution.py:807
  113.1 37.3 %collective-permute-start.18 = (bf16[2,3,216,768]{3,2,1,0:T(8,128)(2,1)}, bf16[2,3,216,768]{3,2,1,0:T(8,128)(2,1)}, u32[]{:S(2)}, u32[]{:S(2)}) collective-permute-start(bf16[2,3,216,768]{3,2,1,0:T(8,128)(2,1)} %collective-permute-done.17.refs_13_), channel_id=1, source_target_pairs={{0,4},{4,0},{8,12},{12,8},{16,20},{20,16},{24,28},{28,24},{1,5},{5... | collective-permute-start | bytes 5971976 | tf_op jit(solution)/shard_map/ppermute | solution.py:797
  114.9 18.4 %collective-permute-start.14 = (bf16[256,384]{1,0:T(8,128)(2,1)S(1)}, bf16[256,384]{1,0:T(8,128)(2,1)S(1)}, u32[]{:S(2)}, u32[]{:S(2)}) collective-permute-start(bf16[256,384]{1,0:T(8,128)(2,1)S(1)} %copy-done.29), channel_id=1, source_target_pairs={{0,8},{4,12},{8,0},{12,4},{16,24},{20,28},{24,16},{28,20},{1,9},{5... | collective-permute-start | bytes 589832 | tf_op jit(solution)/shard_map/ppermute | solution.py:792
  116.3 18.9 %collective-permute-start.15 = (bf16[256,384]{1,0:T(8,128)(2,1)S(1)}, bf16[256,384]{1,0:T(8,128)(2,1)S(1)}, u32[]{:S(2)}, u32[]{:S(2)}) collective-permute-start(bf16[256,384]{1,0:T(8,128)(2,1)S(1)} %copy-done.28), channel_id=1, source_target_pairs={{0,16},{4,20},{8,24},{12,28},{16,0},{20,4},{24,8},{28,12},{1,17},{... | collective-permute-start | bytes 589832 | tf_op jit(solution)/shard_map/ppermute | solution.py:792
  117.9 17.4 %collective-permute-start.16 = (bf16[256,384]{1,0:T(8,128)(2,1)S(1)}, bf16[256,384]{1,0:T(8,128)(2,1)S(1)}, u32[]{:S(2)}, u32[]{:S(2)}) collective-permute-start(bf16[256,384]{1,0:T(8,128)(2,1)S(1)} %copy-done.27), channel_id=1, source_target_pairs={{0,24},{4,28},{8,16},{12,20},{16,8},{20,12},{24,0},{28,4},{1,25},{... | collective-permute-start | bytes 589832 | tf_op jit(solution)/shard_map/ppermute | solution.py:792
  133.3 17.1 %collective-permute-start.20 = (bf16[3,216,768]{2,1,0:T(8,128)(2,1)}, bf16[3,216,768]{2,1,0:T(8,128)(2,1)}, u32[]{:S(2)}, u32[]{:S(2)}) collective-permute-start(bf16[3,216,768]{2,1,0:T(8,128)(2,1)} %collective-permute-done.19.refs_15_), channel_id=1, source_target_pairs={{0,4},{4,0},{8,12},{12,8},{16,20},{20,16},{24,28},{28,24},{1,5},{5... | collective-permute-start | bytes 2985992 | tf_op jit(solution)/shard_map/ppermute | solution.py:797
  200.0 54.6 %collective-permute-start.25 = (bf16[4,864,768]{2,1,0:T(8,128)(2,1)}, bf16[4,864,768]{2,1,0:T(8,128)(2,1)}, u32[]{:S(2)}, u32[]{:S(2)}) collective-permute-start(bf16[4,864,768]{2,1,0:T(8,128)(2,1)} %get-tuple-element.106), channel_id=1, source_target_pairs={{0,4},{4,0},{8,12},{12,8},{16,20},{20,16},{24,28},{28,24},{1,5},{5... | collective-permute-start | bytes 15925256 | tf_op jit(solution)/shard_map/ppermute | solution.py:797
  254.5 69.6 %collective-permute-start.28 = (bf16[384,576]{0,1:T(8,128)(2,1)}, bf16[384,576]{0,1:T(8,128)(2,1)}, u32[]{:S(2)}, u32[]{:S(2)}) collective-permute-start(bf16[384,576]{0,1:T(8,128)(2,1)} %collective-permute-done.27), channel_id=1, source_target_pairs={{0,4},{4,0},{8,12},{12,8},{16,20},{20,16},{24,28},{28,24},{1,5},{5... | collective-permute-start | bytes 1327112 | tf_op jit(solution)/shard_map/ppermute | solution.py:797
  260.8 47.3 %collective-permute-start.32 = (bf16[2,432,768]{2,1,0:T(8,128)(2,1)}, bf16[2,432,768]{2,1,0:T(8,128)(2,1)}, u32[]{:S(2)}, u32[]{:S(2)}) collective-permute-start(bf16[2,432,768]{2,1,0:T(8,128)(2,1)} %pad_maximum_fusion.1), channel_id=1, source_target_pairs={{0,8},{4,12},{8,0},{12,4},{16,24},{20,28},{24,16},{28,20},{1,9},{5... | collective-permute-start | bytes 3981320 | tf_op jit(solution)/shard_map/ppermute | solution.py:792
  262.6 48.4 %collective-permute-start.33 = (bf16[2,432,768]{2,1,0:T(8,128)(2,1)}, bf16[2,432,768]{2,1,0:T(8,128)(2,1)}, u32[]{:S(2)}, u32[]{:S(2)}) collective-permute-start(bf16[2,432,768]{2,1,0:T(8,128)(2,1)} %pad_maximum_fusion.3), channel_id=1, source_target_pairs={{0,16},{4,20},{8,24},{12,28},{16,0},{20,4},{24,8},{28,12},{1,17},{... | collective-permute-start | bytes 3981320 | tf_op jit(solution)/shard_map/ppermute | solution.py:792
  310.2 16.7 %collective-permute-start.44 = (bf16[432,768]{1,0:T(8,128)(2,1)}, bf16[432,768]{1,0:T(8,128)(2,1)}, u32[]{:S(2)}, u32[]{:S(2)}) collective-permute-start(bf16[432,768]{1,0:T(8,128)(2,1)} %fusion.17), channel_id=1, source_target_pairs={{0,16},{4,20},{8,24},{12,28},{16,0},{20,4},{24,8},{28,12},{1,17},{... | collective-permute-start | bytes 1990664 | tf_op jit(solution)/shard_map/ppermute | solution.py:792
  313.1 15.4 %collective-permute-start.45 = (bf16[432,768]{1,0:T(8,128)(2,1)}, bf16[432,768]{1,0:T(8,128)(2,1)}, u32[]{:S(2)}, u32[]{:S(2)}) collective-permute-start(bf16[432,768]{1,0:T(8,128)(2,1)} %fusion.19), channel_id=1, source_target_pairs={{0,8},{4,12},{8,0},{12,4},{16,24},{20,28},{24,16},{28,20},{1,9},{5... | collective-permute-start | bytes 1990664 | tf_op jit(solution)/shard_map/ppermute | solution.py:792
  338.1 37.0 %collective-permute-start.36 = (bf16[512,576]{0,1:T(8,128)(2,1)}, bf16[512,576]{0,1:T(8,128)(2,1)}, u32[]{:S(2)}, u32[]{:S(2)}) collective-permute-start(bf16[512,576]{0,1:T(8,128)(2,1)} %copy.141), channel_id=1, source_target_pairs={{0,24},{4,28},{8,16},{12,20},{16,8},{20,12},{24,0},{28,4},{1,25},{... | collective-permute-start | bytes 1769480 | tf_op jit(solution)/shard_map/ppermute | solution.py:792
  341.5 30.7 %collective-permute-start.35 = (bf16[512,576]{0,1:T(8,128)(2,1)}, bf16[512,576]{0,1:T(8,128)(2,1)}, u32[]{:S(2)}, u32[]{:S(2)}) collective-permute-start(bf16[512,576]{0,1:T(8,128)(2,1)} %copy.140), channel_id=1, source_target_pairs={{0,16},{4,20},{8,24},{12,28},{16,0},{20,4},{24,8},{28,12},{1,17},{... | collective-permute-start | bytes 1769480 | tf_op jit(solution)/shard_map/ppermute | solution.py:792
  343.8 24.9 %collective-permute-start.47 = (bf16[216,768]{1,0:T(8,128)(2,1)S(1)}, bf16[216,768]{1,0:T(8,128)(2,1)}, u32[]{:S(2)}, u32[]{:S(2)}) collective-permute-start(bf16[216,768]{1,0:T(8,128)(2,1)S(1)} %pad_maximum_fusion.11), channel_id=1, source_target_pairs={{0,2},{1,3},{2,0},{3,1},{4,6},{5,7},{6,4},{7,5},{8,10},{9,11},{10,... | collective-permute-start | bytes 995336 | tf_op jit(solution)/shard_map/ppermute | solution.py:804
  344.7 24.1 %collective-permute-start.46 = (bf16[216,768]{1,0:T(8,128)(2,1)}, bf16[216,768]{1,0:T(8,128)(2,1)}, u32[]{:S(2)}, u32[]{:S(2)}) collective-permute-start(bf16[216,768]{1,0:T(8,128)(2,1)} %pad_maximum_fusion.10), channel_id=1, source_target_pairs={{0,1},{1,0},{2,3},{3,2},{4,5},{5,4},{6,7},{7,6},{8,9},{9,8},{10,11... | collective-permute-start | bytes 995336 | tf_op jit(solution)/shard_map/ppermute | solution.py:804
  358.5 15.7 %collective-permute-start.34 = (bf16[512,576]{0,1:T(8,128)(2,1)S(1)}, bf16[512,576]{0,1:T(8,128)(2,1)S(1)}, u32[]{:S(2)}, u32[]{:S(2)}) collective-permute-start(bf16[512,576]{0,1:T(8,128)(2,1)S(1)} %copy-done.18), channel_id=1, source_target_pairs={{0,8},{4,12},{8,0},{12,4},{16,24},{20,28},{24,16},{28,20},{1,9},{5... | collective-permute-start | bytes 1769480 | tf_op jit(solution)/shard_map/ppermute | solution.py:792
  (65 other events, 551.9 us)
